TPU v7x, 256 devices: a whole 4x4x8 slice. The times are simulated.
256 devices in a mesh: row: 16 (over z, core), col: 16 (over y, x).
Axes of the slice: x: 4, y: 4, z: 8, core: 2. Of those that a mesh axis runs over, the one named last changes fastest.
Arguments:
- inverse: float32 [5, 16, 5, 16, 256, 256], P(None, 'row', None, 'col')
- struct_first: int32 [32], replicated, may hold values from 0 to 79, as said below
- struct_second: int32 [16], replicated, may hold values from 0 to 79, as said below
- factor_first: float32 [32, 256, 256], P('row'), may hold values from -0.25 to 0.25
- factor_second: float32 [16, 256, 256], P('row'), may hold values from -0.25 to 0.25
- link_factor: float32 [256, 256], replicated, may hold values from -0.375 to 0.375
- dinv_first: float32 [256, 256], replicated, may hold values from -6 to 6
- dinv_second: float32 [256, 256], replicated, may hold values from -6 to 6
Outputs:
- column_first: float32 [5, 16, 256, 256], P(None, 'row', None, 'col')
- diag_first: float32 [256, 256], P(None, 'col')
- column_second: float32 [5, 16, 256, 256], P(None, 'row', None, 'col')
- link_second: float32 [256, 256], P(None, 'col')
- diag_second: float32 [256, 256], P(None, 'col')
Inputs may be any that keep to these rules, and one draw needn't show every extreme that they name: `struct_first`: distinct tile ids. `struct_second`: distinct tile ids, each of them also in struct_first.
All inputs are finite; a program needn't handle non-finite values.
Results may differ from a plain program's by a relative error of at most 0.0001.
Values sent between devices are 32-bit elements; how exact they have to be, the bound alone decides.
A program may use at most 128 MiB of HBM per device.

v0:
```python
import jax
import jax.numpy as jnp
from jax import lax
from jax.sharding import PartitionSpec as P

PRECISE = lax.Precision.HIGHEST


def body(
    inverse,
    struct_first,
    struct_second,
    factor_first,
    factor_second,
    link_factor,
    dinv_first,
    dinv_second,
):
    grid_rows = lax.axis_size("row")
    grid_cols = lax.axis_size("col")
    my_row = lax.axis_index("row")
    my_col = lax.axis_index("col")
    tile_rows, _, tile_cols, _, extent, _ = inverse.shape
    local_inv = inverse.reshape(tile_rows, tile_cols, extent, extent)
    col_width = extent // grid_cols
    offset = my_col * col_width
    col_tiles = jnp.arange(tile_cols, dtype=jnp.int32) * grid_cols + my_col
    row_tiles = jnp.arange(tile_rows, dtype=jnp.int32) * grid_rows + my_row

    def route(factor, tile_ids):
        block_in = lax.all_gather(factor, "row", axis=0, tiled=True)
        pick_col = (tile_ids[None, :] == col_tiles[:, None]).astype(jnp.float32)
        pick_row = (tile_ids[None, :] == row_tiles[:, None]).astype(jnp.float32)
        col_sel = jnp.einsum("bj,jxy->bxy", pick_col, block_in, precision=PRECISE)
        row_sel = jnp.einsum("aj,jxy->axy", pick_row, block_in, precision=PRECISE)
        return (col_sel, row_sel)

    def reduce_cols(stacked):
        summed = lax.psum(stacked, "col")
        return lax.dynamic_slice_in_dim(summed, offset, col_width, 2)

    col_first, row_first = route(factor_first, struct_first)
    product_first = jnp.einsum("abxy,byz->axz", local_inv, col_first, precision=PRECISE)
    panel_first = reduce_cols(product_first)
    owned_first = jnp.any(row_tiles[:, None] == struct_first[None, :], axis=1).astype(jnp.float32)
    column_first = -owned_first[:, None, None] * panel_first
    diag_terms = jnp.einsum("axy,axz->yz", row_first, panel_first, precision=PRECISE)
    diag_first = lax.dynamic_slice_in_dim(dinv_first, offset, col_width, 1) + lax.psum(
        diag_terms, "row"
    )
    col_second, row_second = route(factor_second, struct_second)
    link_rows = lax.dynamic_slice_in_dim(link_factor, offset, col_width, 0)
    product_second = jnp.einsum("abxy,byz->axz", local_inv, col_second, precision=PRECISE)
    product_second = product_second + jnp.einsum(
        "axw,wz->axz", column_first, link_rows, precision=PRECISE
    )
    link_term = jnp.dot(
        diag_first, link_rows, precision=PRECISE, preferred_element_type=jnp.float32
    )
    reduced = reduce_cols(jnp.concatenate([product_second, link_term[None]], axis=0))
    panel_second = reduced[:tile_rows]
    join_share = reduced[tile_rows]
    owned_second = jnp.any(row_tiles[:, None] == struct_second[None, :], axis=1).astype(jnp.float32)
    column_second = -owned_second[:, None, None] * panel_second
    turned_part = jnp.einsum("axw,axz->wz", column_first, row_second, precision=PRECISE)
    second_terms = jnp.einsum("axy,axz->yz", row_second, panel_second, precision=PRECISE)
    turned_sum, second_sum = lax.psum((turned_part, second_terms), "row")
    turned = lax.all_to_all(turned_sum, "col", split_axis=1, concat_axis=0, tiled=True)
    joined = turned + join_share
    link_second = -joined
    diag_second = lax.dynamic_slice_in_dim(dinv_second, offset, col_width, 1) + second_sum
    diag_second = diag_second + jnp.dot(
        link_factor.T, joined, precision=PRECISE, preferred_element_type=jnp.float32
    )
    out_shape = (tile_rows, 1, extent, col_width)
    return (
        column_first.reshape(out_shape),
        diag_first,
        column_second.reshape(out_shape),
        link_second,
        diag_second,
    )


def solution(mesh):
    placed = (
        P(None, "row", None, "col", None, None),
        P(),
        P(),
        P("row", None, None),
        P("row", None, None),
        P(),
        P(),
        P(),
    )
    return jax.shard_map(
        body,
        mesh=mesh,
        in_specs=placed,
        out_specs=(
            P(None, "row", None, "col"),
            P(None, "col"),
            P(None, "row", None, "col"),
            P(None, "col"),
            P(None, "col"),
        ),
        check_vma=False,
    )
```

profile of v0, /device:TPU:2, one launch (start us, length us, event | category | flops | bytes accessed | tf_op | source)
XLA Modules:
  0.0 435.4 jit_solution(15003734028828694786)
XLA Ops:
  10.7 58.0 %all-gather.3.cloned.1.call-done = f32[32,256,256]{2,1,0:T(8,128)} async-done(((f32[2,256,256]{2,1,0:T(8,128)}), f32[32,256,256]{2,1,0:T(8,128)}) %all-gather.3.cloned.1.call-update) | async-done | bytes 8388624 | tf_op jit(solution)/shard_map/all_gather | solution.py:31
  68.7 10.6 %fusion.2 = f32[5,256,256]{2,0,1:T(8,128)S(1)} fusion(f32[32,256,256]{2,1,0:T(8,128)} %all-gather.3.cloned.1.call-done, s32[32]{0:T(128)} %param.9, s32[5]{0:T(128)S(1)} %fusion.62), kind=kOutput, calls=%fused_computation.2 | convolution fusion | flops 125829280 | bytes 9699476 | tf_op jit(solution)/shard_map/bj,jxy->bxy/dot_general | solution.py:34
  79.3 1.5 copy.35
  80.8 9.9 %fusion.12 = f32[5,256,256]{1,2,0:T(8,128)} fusion(f32[5,1,5,1,256,256]{5,4,3,2,1,0:T(8,128)} %param.8, f32[5,256,256]{1,2,0:T(8,128)} %copy.35), kind=kOutput, calls=%fused_computation.13 | convolution fusion | flops 5033164800 | bytes 9175040 | tf_op jit(solution)/shard_map/abxy,byz->axz/dot_general | solution.py:43
  90.8 10.8 %all-reduce.6.cloned.1.call-start = ((), (), s32[]{:S(2)}) async-start(), calls=%async_computation.4 | async-start | bytes 3145728 | tf_op jit(solution)/shard_map/psum | solution.py:39
  101.6 9.4 %all-gather.5.cloned.1.call-done = f32[16,256,256]{2,1,0:T(8,128)} async-done(((f32[1,256,256]{2,1,0:T(8,128)}), f32[16,256,256]{2,1,0:T(8,128)}) %all-gather.5.cloned.1.call-update) | async-done | bytes 4194320 | tf_op jit(solution)/shard_map/all_gather | solution.py:31
  111.0 5.8 %fusion.10 = f32[5,256,256]{2,0,1:T(8,128)S(1)} fusion(f32[16,256,256]{2,1,0:T(8,128)} %all-gather.5.cloned.1.call-done, s32[16]{0:T(128)S(1)} %copy-done.4, s32[5]{0:T(128)S(1)} %fusion.62), kind=kOutput, calls=%fused_computation.10 | convolution fusion | flops 62914640 | bytes 5505108 | tf_op jit(solution)/shard_map/bj,jxy->bxy/dot_general | solution.py:34
  116.8 1.5 copy.40
  118.3 10.0 %fusion.15 = f32[5,256,256]{1,2,0:T(8,128)} fusion(f32[5,1,5,1,256,256]{5,4,3,2,1,0:T(8,128)} %param.8, f32[5,256,256]{1,2,0:T(8,128)} %copy.40), kind=kOutput, calls=%fused_computation.14 | convolution fusion | flops 5033164800 | bytes 9175040 | tf_op jit(solution)/shard_map/abxy,byz->axz/dot_general | solution.py:53
  128.3 10.7 %fusion = f32[5,256,256]{2,0,1:T(8,128)S(1)} fusion(f32[32,256,256]{2,1,0:T(8,128)} %all-gather.3.cloned.1.call-done, s32[32]{0:T(128)S(1)} %copy-done.3, s32[5]{0:T(128)S(1)} %fusion.63), kind=kOutput, calls=%fused_computation | convolution fusion | flops 125829280 | bytes 9699476 | tf_op jit(solution)/shard_map/aj,jxy->axy/dot_general | solution.py:35
  139.0 71.3 %all-reduce.4.cloned.1.call-done = f32[5,256,256]{1,2,0:T(8,128)} async-done(((f32[5,256,256]{1,2,0:T(8,128)}), f32[5,256,256]{1,2,0:T(8,128)}) %all-reduce.4.cloned.1.call-update) | async-done | bytes 1310736 | tf_op jit(solution)/shard_map/psum | solution.py:39
  210.4 1.9 fusion.22
  212.3 46.3 %psum.36 = f32[256,16]{0,1:T(8,128)S(1)} all-reduce(f32[256,16]{0,1:T(8,128)S(1)} %fusion.22), channel_id=1, replica_groups=mesh['row'=16,'col'=16] {'row'}, use_global_device_ids=true, to_apply=%region_2.0 | all-reduce | flops 4096 | bytes 32768 | tf_op jit(solution)/shard_map/psum | solution.py:48
  259.0 2.6 convolution_add_fusion
  264.2 5.8 %fusion.8 = f32[5,256,256]{2,0,1:T(8,128)S(1)} fusion(f32[16,256,256]{2,1,0:T(8,128)} %all-gather.5.cloned.1.call-done, s32[16]{0:T(128)S(1)} %copy-done.4, s32[5]{0:T(128)S(1)} %fusion.63), kind=kOutput, calls=%fused_computation.8 | convolution fusion | flops 62914640 | bytes 5505108 | tf_op jit(solution)/shard_map/aj,jxy->axy/dot_general | solution.py:35
  270.0 1.6 fusion.31
  271.6 3.2 fusion.27
  274.9 86.3 %all-reduce.6.cloned.1.call-done = f32[6,256,256]{1,2,0:T(8,128)} async-done(((f32[6,256,256]{1,2,0:T(8,128)}), f32[6,256,256]{1,2,0:T(8,128)}) %all-reduce.6.cloned.1.call-update) | async-done | bytes 1572880 | tf_op jit(solution)/shard_map/psum | solution.py:39
  361.2 1.9 convolution_bitcast_fusion.1
  363.1 48.2 %all-reduce = (f32[16,16,16]{0,2,1:T(8,128)S(1)}, f32[256,16]{0,1:T(8,128)S(1)}) all-reduce(f32[16,16,16]{0,2,1:T(8,128)S(1)} %bitcast.78, f32[256,16]{0,1:T(8,128)S(1)} %convolution_bitcast_fusion.1), channel_id=1, replica_groups=mesh['row'=16,'col'=16] {'row'}, use_global_device_ids=true, to_apply=%region_5.0 | all-reduce | flops 8192 | bytes 65536 | tf_op jit(solution)/shard_map/psum | solution.py:67
  412.0 5.9 %all-to-all-start = ((f32[16,1,256]{2,1,0:T(1,128)}), f32[16,1,256]{2,1,0:T(1,128)S(1)}, u32[]{:S(2)}, u32[]{:S(2)}) async-start(f32[16,1,256]{2,1,0:T(1,128)} %reshape.57), calls=%async_computation | async-start | bytes 32768 | tf_op jit(solution)/shard_map/all_to_all | solution.py:68
  417.9 1.6 multiply_bitcast_fusion
  419.5 4.6 %all-to-all-done = f32[16,1,256]{2,1,0:T(1,128)S(1)} async-done(((f32[16,1,256]{2,1,0:T(1,128)}), f32[16,1,256]{2,1,0:T(1,128)S(1)}, u32[]{:S(2)}, u32[]{:S(2)}) %all-to-all-start) | async-done | bytes 16416 | tf_op jit(solution)/shard_map/all_to_all | solution.py:68
  426.9 1.6 fusion.25
  (38 shorter events, 9.9 us)
Async XLA Ops:
  7.2 251.4 %copy-start = (f32[256,256]{1,0:T(8,128)S(1)}, f32[256,256]{1,0:T(8,128)}, u32[]{:S(2)}) copy-start(f32[256,256]{1,0:T(8,128)} %param.13) | copy-start | bytes 786436
  7.2 61.5 %all-gather.3.cloned.1.call-start = ((), (), s32[]{:S(2)}) async-start(), calls=%async_computation.1 | async-start | bytes 8912896 | tf_op jit(solution)/shard_map/all_gather | solution.py:31
  7.9 103.0 %all-gather.5.cloned.1.call-start = ((), (), s32[]{:S(2)}) async-start(), calls=%async_computation.3 | async-start | bytes 4456448 | tf_op jit(solution)/shard_map/all_gather | solution.py:31
  8.7 201.7 %all-reduce.4.cloned.1.call-start = ((), (), s32[]{:S(2)}) async-start(), calls=%async_computation.2 | async-start | bytes 2621440 | tf_op jit(solution)/shard_map/psum | solution.py:39
  80.8 30.1 %copy-start.4 = (s32[16]{0:T(128)S(1)}, s32[16]{0:T(128)}, u32[]{:S(2)}) copy-start(s32[16]{0:T(128)} %param.10) | copy-start | bytes 196
  90.8 270.4 %all-reduce.6.cloned.1.call-start = ((), (), s32[]{:S(2)}) async-start(), calls=%async_computation.4 | async-start | bytes 3145728 | tf_op jit(solution)/shard_map/psum | solution.py:39
  118.3 10.0 %copy-start.3 = (s32[32]{0:T(128)S(1)}, s32[32]{0:T(128)}, u32[]{:S(2)}) copy-start(s32[32]{0:T(128)} %param.9) | copy-start | bytes 388
  258.5 4.3 copy-start.1
  262.9 1.0 copy-start.2
  412.0 12.1 %all-to-all-start = ((f32[16,1,256]{2,1,0:T(1,128)}), f32[16,1,256]{2,1,0:T(1,128)S(1)}, u32[]{:S(2)}, u32[]{:S(2)}) async-start(f32[16,1,256]{2,1,0:T(1,128)} %reshape.57), calls=%async_computation | async-start | bytes 32768 | tf_op jit(solution)/shard_map/all_to_all | solution.py:68
Sparse Core Ops, SparseCore 0:
  9.8 58.7 all-gather.2
  70.5 40.4 all-gather.4
  114.2 96.1 all-reduce.3
  263.0 98.1 all-reduce.5
where the time goes:
time: 444 us; the launch traced here: 435 us
  waiting for transfers between devices  231 us (52%)
  blocking collectives  94.4 us (21%)
  matrix products  64.5 us (15%)
  starting transfers between devices  16.8 us (4%)
  between operations  14.3 us (3%)
  other arithmetic  7.53 us (2%)
  local copies, waits for them, and re-layouts  6.73 us (2%)
    psum x2, waiting for transfers between devices, reduce_cols(): summed = lax.psum(stacked, 'col')  158 us
    all_gather x2, waiting for transfers between devices, route(): block_in = lax.all_gather(factor, 'row', axis=0, tiled=True)  67.4 us
    psum x1, blocking collectives, body(): turned_sum, second_sum = lax.psum((turned_part, second_terms), 'row')  48.2 us
    psum x1, blocking collectives, body(): lax.psum(diag_terms, 'row')  46.3 us
    dot_general x2, matrix products, route(): row_sel = jnp.einsum('aj,jxy->axy', pick_row, block_in, precision=PRECISE)  16.6 us
    dot_general x2, matrix products, route(): col_sel = jnp.einsum('bj,jxy->bxy', pick_col, block_in, precision=PRECISE)  16.5 us
    psum x2, starting transfers between devices, reduce_cols(): summed = lax.psum(stacked, 'col')  10.8 us
    dot_general x1, matrix products, body(): jnp.einsum('abxy,byz->axz', local_inv, col_second, precision=PRECISE)  9.96 us
  transfers between devices with their start and end apart: 5, of which 5 were waited for; matrix products, arithmetic and copies ran while one was open for 15% of the time, Pallas kernels for 0%

commit v1 on v0

v1 whole, which is shorter than its diff:
```python
import functools

import jax
import jax.numpy as jnp
from jax import lax
from jax.experimental import pallas as pl
from jax.experimental.pallas import tpu as pltpu
from jax.sharding import PartitionSpec as P

MESH = pl.DeviceIdType.MESH
SIDE = 4
F32 = jnp.float32
BF16 = jnp.bfloat16


def split(v):
    hi = v.astype(BF16)
    return hi, (v - hi.astype(F32)).astype(BF16)


def mm(p, q):
    return jnp.dot(p, q, preferred_element_type=F32)


def dot3(p, q):
    ph, plo = split(p)
    qh, qlo = split(q)
    return mm(ph, qh) + (mm(ph, qlo) + mm(plo, qh))


def kernel(
    nr, nc, na, ns, f1, f2, width,
    tab, inv, fac1, fac2, link, dinv1, dinv2,
    o1, o2, o3,
    a_v, l_v, d1_v, d2_v, lt_v,
    pf, pg, pf2, pg2, st, cw, wh, wl, acc,
    hop, hopped, fb, ysum, zin, xb, frb, grb,
    st2, rb, m_v, rx, n_v, q_v, s_v, u_v, w_v,
    ld, lds, s1, pfr, pgr, pxs, pxr, bs, br, cs, cr,
    r1s, r1r, r2s, fbr, zs, zr, ts, tr, es, er, qs, qr, us, ur, vs, vr,
):
    r = lax.axis_index("row")
    c = lax.axis_index("col")
    k = lax.rem(r, 2)
    z = r // 2
    nz = nr // 2
    y = c // SIDE
    x = lax.rem(c, SIDE)
    mate = z * 2 + (1 - k)

    def remote(src, dst, ss, rs, row, col):
        return pltpu.make_async_remote_copy(
            src_ref=src, dst_ref=dst, send_sem=ss, recv_sem=rs,
            device_id=(row, col), device_id_type=MESH,
        )

    def take(ref, sem):
        pltpu.make_async_copy(ref, ref, sem).wait()

    def load_a(b):
        return pltpu.make_async_copy(inv.at[:, b], a_v.at[:, b], ld.at[b])

    small = [
        pltpu.make_async_copy(link, l_v, lds.at[0]),
        pltpu.make_async_copy(dinv1, d1_v, lds.at[1]),
        pltpu.make_async_copy(dinv2, d2_v, lds.at[2]),
    ]
    barrier = pltpu.get_barrier_semaphore()

    def greet_row(d, carry):
        pl.semaphore_signal(barrier, inc=1, device_id=(lax.rem(r + d, nr), c), device_id_type=MESH)
        return carry

    def greet_col(d, carry):
        pl.semaphore_signal(barrier, inc=1, device_id=(r, lax.rem(c + d, nc)), device_id_type=MESH)
        return carry

    lax.fori_loop(1, nr, greet_row, 0)
    lax.fori_loop(1, nc, greet_col, 0)
    row8 = pl.multiple_of(128 * k + 8 * c, 8)
    pltpu.make_async_copy(fac1.at[:, pl.ds(row8, 8), :], pf.at[pl.ds(r * f1, f1)], pfr).start()
    pltpu.make_async_copy(fac2.at[:, pl.ds(row8, 8), :], pg.at[pl.ds(r * f2, f2)], pgr).start()
    for cp in small:
        cp.start()
    for b in range(ns):
        load_a(b).start()
    pl.semaphore_wait(barrier, nr + nc - 2)

    def send_pieces(fac, buf, count, rsem):
        def go(d, carry):
            r2 = lax.rem(r + d, nr)
            k2 = lax.rem(r2, 2)
            rows = pl.multiple_of(128 * k2 + 8 * c, 8)
            remote(
                fac.at[:, pl.ds(rows, 8), :], buf.at[pl.ds(r * count, count)], s1, rsem, r2, c
            ).start()
            return carry

        lax.fori_loop(1, nr, go, 0)

    send_pieces(fac1, pf, f1, pfr)
    send_pieces(fac2, pg, f2, pgr)

    for cp in small:
        cp.wait()
    first = jnp.where(jnp.logical_and(r == 0, c == 0), 1.0, 0.0).astype(F32)
    lt_v[...] = jnp.transpose(l_v[...])
    d1_v[...] = jnp.transpose(d1_v[...]) * first
    d2_v[...] = jnp.transpose(d2_v[...]) * first

    take(pf, pfr)
    take(pg, pgr)
    swap_f = remote(pf, pf2, pxs.at[0], pxr.at[0], mate, c)
    swap_g = remote(pg, pg2, pxs.at[1], pxr.at[1], mate, c)

    def pack(b, carry):
        def one(c2, carry2):
            j1 = tab[0, b * nc + c2]
            j2 = tab[1, b * nc + c2]
            v1 = pf[jnp.maximum(j1, 0)]
            v2 = pg[jnp.maximum(j2, 0)]
            st[c2, b, 0] = jnp.where(j1 >= 0, v1, 0.0)
            st[c2, b, 1] = jnp.where(j2 >= 0, v2, 0.0)
            return carry2

        lax.fori_loop(0, nc, one, 0)
        pltpu.make_async_copy(st.at[c, b], cw.at[b, :, k, c], br.at[b]).start()

        def go(d, carry2):
            c2 = lax.rem(c + d, nc)
            remote(st.at[c2, b], cw.at[b, :, k, c], bs, br.at[b], r, c2).start()
            return carry2

        lax.fori_loop(1, nc, go, 0)
        return carry

    lax.fori_loop(0, ns, pack, 0)
    swap_f.start()
    swap_g.start()

    def ring(h):
        if h == 0:
            return x, y * SIDE + lax.rem(x + 1, SIDE), y * SIDE + lax.rem(x + SIDE - 1, SIDE)
        return y, lax.rem(y + 1, SIDE) * SIDE + x, lax.rem(y + SIDE - 1, SIDE) * SIDE + x

    half = SIDE // 2

    def part(a, h, who, lo, n):
        if h == 0:
            return acc.at[a, 0, pl.ds(lo, n), who]
        return acc.at[a, 1, who, pl.ds(lo, n)]

    def step_one(a):
        for h in range(2):
            u, right, left = ring(h)
            up, down, far = lax.rem(u + 1, SIDE), lax.rem(u + SIDE - 1, SIDE), lax.rem(u + 2, SIDE)
            remote(part(a, h, far, 0, half), hop.at[h, 0, a], r1s, r1r.at[h, 0, a], r, right).start()
            remote(part(a, h, far, half, half), hop.at[h, 1, a], r1s, r1r.at[h, 1, a], r, left).start()
            remote(
                part(a, h, up, half, half), fb.at[h, 0, a, pl.ds(half, half)], r1s, fbr.at[h, 0, a], r, right
            ).start()
            remote(
                part(a, h, down, 0, half), fb.at[h, 1, a, pl.ds(0, half)], r1s, fbr.at[h, 1, a], r, left
            ).start()

    def exchange(b):
        return remote(cw.at[b, :, k], cw.at[b, :, k], cs, cr.at[b], mate, c)

    def slot(b):
        ff = cw[b, 0].reshape(256, 256)
        gg = cw[b, 1].reshape(256, 256)
        hh = gg - dot3(ff, l_v[...])
        fh, fl = split(ff)
        hhi, hlo = split(hh)
        wh[:, 0:256] = fh
        wl[:, 0:256] = fl
        wh[:, 256:512] = hhi
        wl[:, 256:512] = hlo
        load_a(b).wait()

        def rowstep(a, carry):
            ah, al = split(a_v[a, b])
            got = mm(ah, wh[...]) + (mm(ah, wl[...]) + mm(al, wh[...]))
            got = got.reshape(2, SIDE, SIDE, 8, 512)

            @pl.when(b == 0)
            def _():
                acc[a] = got

            @pl.when(b > 0)
            def _():
                acc[a] += got

            @pl.when(b == ns - 1)
            def _():
                step_one(a)

            return carry

        lax.fori_loop(0, na, rowstep, 0)

    def slots(b, carry):
        @pl.when(b < ns)
        def _():
            take(cw.at[b, :, k], br.at[b])
            exchange(b).start()

        @pl.when(b > 0)
        def _():
            take(cw.at[b - 1, :, k], cr.at[b - 1])
            slot(b - 1)

        return carry

    lax.fori_loop(0, ns + 1, slots, 0)

    def step_two(a, carry):
        for h in range(2):
            u, right, left = ring(h)
            up, down = lax.rem(u + 1, SIDE), lax.rem(u + SIDE - 1, SIDE)
            take(hop.at[h, 0, a], r1r.at[h, 0, a])
            hopped[h, 0, a] = hop[h, 0, a] + part(a, h, up, 0, half)[...]
            remote(
                hopped.at[h, 0, a], fb.at[h, 0, a, pl.ds(0, half)], r2s, fbr.at[h, 0, a], r, right
            ).start()
            take(hop.at[h, 1, a], r1r.at[h, 1, a])
            hopped[h, 1, a] = hop[h, 1, a] + part(a, h, down, half, half)[...]
            remote(
                hopped.at[h, 1, a], fb.at[h, 1, a, pl.ds(half, half)], r2s, fbr.at[h, 1, a], r, left
            ).start()
        return carry

    lax.fori_loop(0, na, step_two, 0)

    swap_f.wait()
    swap_g.wait()
    frb[...] = jnp.zeros_like(frb)
    grb[...] = jnp.zeros_like(grb)
    xb[...] = jnp.zeros_like(xb)
    for a in range(na):
        j1 = tab[0, a * nr + r]
        j2 = tab[1, a * nr + r]
        for h in range(2):
            lo = a * 16 + h * 8
            i1, i2 = jnp.maximum(j1, 0), jnp.maximum(j2, 0)
            frb[lo:lo + 8, :] = jnp.where(j1 >= 0, jnp.where(k == h, pf[i1], pf2[i1]), 0.0)
            grb[lo:lo + 8, :] = jnp.where(j2 >= 0, jnp.where(k == h, pg[i2], pg2[i2]), 0.0)

    def second(a, carry):
        for h in range(2):
            u = ring(h)[0]
            take(fb.at[h, 0, a], fbr.at[h, 0, a])
            take(fb.at[h, 1, a], fbr.at[h, 1, a])
            ysum[h, a] = part(a, h, u, 0, SIDE)[...] + (fb[h, 0, a] + fb[h, 1, a])
            v = y if h == 0 else x
            for d in range(1, SIDE):
                v2 = lax.rem(v + d, SIDE)
                col = v2 * SIDE + x if h == 0 else y * SIDE + v2
                remote(ysum.at[h, a, v2], zin.at[h, a, d - 1], zs, zr.at[h, a], r, col).start()
        return carry

    lax.fori_loop(0, na, second, 0)

    def gather(a, carry):
        for h in range(2):
            v = y if h == 0 else x
            take(zin.at[h, a], zr.at[h, a])
            tot = ysum[h, a, v] + (zin[h, a, 0] + zin[h, a, 1] + zin[h, a, 2])
            xb[pl.ds(pl.multiple_of(a * 16 + h * 8, 8), 8), :] = tot
        return carry

    lax.fori_loop(0, na, gather, 0)

    lane = lax.broadcasted_iota(jnp.int32, (16, 128), 1) // 16
    for c2 in range(nc):
        blk, off = c2 // 8, c2 % 8
        for q in range(width // 128):
            val = jnp.zeros((16, 128), F32)
            for g in range(8):
                p = q * 8 + g
                if p < 2 * na:
                    fg, a = p // na, p % na
                    src = xb[a * 16:a * 16 + 16, fg * 256 + blk * 128:fg * 256 + blk * 128 + 128]
                    shift = (16 * (g - off)) % 128
                    if shift:
                        src = pltpu.roll(src, shift, axis=1)
                    val = jnp.where(lane == g, src, val)
            st2[c2, :, :, q * 128:(q + 1) * 128] = val.reshape(2, 8, 128)
    pltpu.make_async_copy(st2.at[c], rb.at[:, c], tr).start()

    def send_cols(d, carry):
        c2 = lax.rem(c + d, nc)
        remote(st2.at[c2], rb.at[:, c], ts, tr, r, c2).start()
        return carry

    lax.fori_loop(1, nc, send_cols, 0)

    x1 = xb[:, 0:256]
    x2 = xb[:, 256:512]
    d1t = dot3(jnp.transpose(x1), frb[...]) + d1_v[...]
    m_v[0] = d1t.reshape(nc, 2, 8, 256)
    jt = dot3(lt_v[...], d1t) - dot3(jnp.transpose(grb[...]), x1)
    m_v[1] = jt.reshape(nc, 2, 8, 256)
    et = dot3(jnp.transpose(x2), grb[...]) + dot3(jt, l_v[...]) + d2_v[...]
    m_v[2] = et.reshape(nc, 2, 8, 256)
    fold = remote(m_v.at[:, :, 1 - k], rx, es, er, mate, c)
    fold.start()
    take(rx, er)
    for t in range(3):
        n_v[t] = m_v[t, :, k] + rx[t]
    pltpu.make_async_copy(n_v.at[:, c], q_v.at[c], qr).start()

    def send_terms(d, carry):
        c2 = lax.rem(c + d, nc)
        remote(n_v.at[:, c2], q_v.at[c], qs, qr, r, c2).start()
        return carry

    lax.fori_loop(1, nc, send_terms, 0)

    take(rb, tr)
    cols = jnp.transpose(rb[...].reshape(256, width))
    for a in range(na):
        j1 = tab[0, a * nr + r]
        j2 = tab[1, a * nr + r]
        o1[a * 16:(a + 1) * 16, :] = jnp.where(j1 >= 0, -cols[a * 16:(a + 1) * 16, :], 0.0)
        lo = (na + a) * 16
        o2[a * 16:(a + 1) * 16, :] = jnp.where(j2 >= 0, -cols[lo:lo + 16, :], 0.0)

    take(q_v, qr)
    tot = q_v[0]
    for i in range(1, nc):
        tot = tot + q_v[i]
    s_v[...] = tot
    pltpu.make_async_copy(s_v, u_v.at[z], ur).start()

    def send_z(d, carry):
        z2 = lax.rem(z + d, nz)
        remote(s_v, u_v.at[z], us, ur, z2 * 2 + k, c).start()
        return carry

    if nz > 1:
        lax.fori_loop(1, nz, send_z, 0)
    take(u_v, ur)
    tot = u_v[0]
    for i in range(1, nz):
        tot = tot + u_v[i]
    w_v[k] = tot
    last = remote(w_v.at[k], w_v.at[k], vs, vr, mate, c)
    last.start()
    take(w_v.at[k], vr)
    for h in range(2):
        o3[0, h * 8:(h + 1) * 8] = w_v[h, 0]
        o3[1, h * 8:(h + 1) * 8] = -w_v[h, 1]
        o3[2, h * 8:(h + 1) * 8] = w_v[h, 2]

    take(pf.at[pl.ds(0, (nr - 1) * f1)], s1)
    take(pg.at[pl.ds(0, (nr - 1) * f2)], s1)
    take(st.at[pl.ds(0, nc - 1)], bs)
    take(cw.at[:, :, 0], cs)
    take(fb, r1s)
    take(hop, r2s)
    take(zin, zs)
    take(rb.at[:, pl.ds(0, nc - 1)], ts)
    take(rx, es)
    take(q_v.at[pl.ds(0, nc - 1)], qs)
    if nz > 1:
        take(u_v.at[pl.ds(0, nz - 1)], us)
    take(w_v.at[0], vs)


def body(inverse, struct_first, struct_second, factor_first, factor_second, link_factor, dinv_first, dinv_second):
    nr = lax.axis_size("row")
    nc = lax.axis_size("col")
    na, _, ns, _, ext, _ = inverse.shape
    f1, f2 = factor_first.shape[0], factor_second.shape[0]
    tiles = max(na * nr, ns * nc)
    ids = jnp.arange(tiles, dtype=jnp.int32)

    def where_is(ids_of):
        n = ids_of.shape[0]
        spot = jnp.arange(1, n + 1, dtype=jnp.int32)
        return jnp.sum(jnp.where(ids[:, None] == ids_of[None, :], spot[None, :], 0), axis=1) - 1

    tab = jnp.stack([where_is(struct_first), where_is(struct_second)])
    width = -(-2 * na * 16 // 128) * 128
    deep = -(-na * 16 // 128) * 128
    any_spec = pl.BlockSpec(memory_space=pl.ANY)
    vm = lambda *s: pltpu.VMEM(s, F32)
    dma = pltpu.SemaphoreType.DMA
    half = SIDE // 2
    o1, o2, o3 = pl.pallas_call(
        functools.partial(kernel, nr, nc, na, ns, f1, f2, width),
        out_shape=(
            jax.ShapeDtypeStruct((na * 16, 256), F32),
            jax.ShapeDtypeStruct((na * 16, 256), F32),
            jax.ShapeDtypeStruct((3, 16, 256), F32),
        ),
        in_specs=[pl.BlockSpec(memory_space=pltpu.SMEM)] + [any_spec] * 6,
        out_specs=(pl.BlockSpec(memory_space=pltpu.VMEM),) * 3,
        scratch_shapes=[
            vm(na, ns, 256, 256), vm(256, 256), vm(256, 256), vm(256, 256), vm(256, 256),
            vm(nr * f1, 8, 256), vm(nr * f2, 8, 256), vm(nr * f1, 8, 256), vm(nr * f2, 8, 256),
            vm(nc, ns, 2, 8, 256), vm(ns, 2, 2, nc, 8, 256),
            pltpu.VMEM((256, 512), BF16), pltpu.VMEM((256, 512), BF16),
            vm(na, 2, SIDE, SIDE, 8, 512),
            vm(2, 2, na, half, 8, 512), vm(2, 2, na, half, 8, 512),
            vm(2, 2, na, SIDE, 8, 512), vm(2, na, SIDE, 8, 512),
            vm(2, na, SIDE - 1, 8, 512),
            vm(deep, 512), vm(deep, 256), vm(deep, 256),
            vm(nc, 2, 8, width), vm(2, nc, 8, width),
            vm(3, nc, 2, 8, 256), vm(3, nc, 8, 256), vm(3, nc, 8, 256), vm(nc, 3, 8, 256),
            vm(3, 8, 256), vm(nr // 2, 3, 8, 256), vm(2, 3, 8, 256),
            dma((ns,)), dma((3,)), dma, dma, dma, dma((2,)), dma((2,)), dma, dma((ns,)), dma, dma((ns,)),
            dma, dma((2, 2, na)), dma, dma((2, 2, na)), dma, dma((2, na)),
            dma, dma, dma, dma, dma, dma, dma, dma, dma, dma,
        ],
        compiler_params=pltpu.CompilerParams(
            collective_id=0, has_side_effects=True, vmem_limit_bytes=56 * 1024 * 1024
        ),
    )(tab, inverse.reshape(na, ns, ext, ext), factor_first, factor_second, link_factor, dinv_first, dinv_second)
    panel = lambda o: jnp.swapaxes(o.reshape(na, 1, 16, 256), 2, 3)
    turn = jnp.swapaxes
    return (panel(o1), turn(o3[0], 0, 1), panel(o2), turn(o3[1], 0, 1), turn(o3[2], 0, 1))


def solution(mesh):
    placed = (
        P(None, "row", None, "col", None, None),
        P(),
        P(),
        P("row", None, None),
        P("row", None, None),
        P(),
        P(),
        P(),
    )
    return jax.shard_map(
        body,
        mesh=mesh,
        in_specs=placed,
        out_specs=(
            P(None, "row", None, "col"),
            P(None, "col"),
            P(None, "row", None, "col"),
            P(None, "col"),
            P(None, "col"),
        ),
        check_vma=False,
    )
```

time: 444 us -> 89.3 us (0.20)
  the two profiles are of different devices: /device:TPU:2 before, /device:TPU:1 now
where the time goes in v1:
time: 89.3 us; the launch traced here: 89 us
  Pallas kernels  81.9 us (92%)
  local copies, waits for them, and re-layouts  4.42 us (5%)
  other arithmetic  2.08 us (2%)
    pallas_call x1, Pallas kernels, body(): pl.pallas_call(functools.partial(kernel, nr, nc, na, ns, f1, f2, width),...  81.9 us
    unnamed x2, local copies, waits for them, and re-layouts  3.05 us

profile of v1, /device:TPU:1, one launch (start us, length us, event | category | flops | bytes accessed | tf_op | source)
XLA Modules:
  0.0 89.0 jit_solution(983222559455444266)
XLA Ops:
  0.6 0.7 select_reduce_fusion
  1.4 0.7 select_reduce_fusion.1
  2.1 0.6 pad_add_fusion.tab
  2.7 81.9 %shard_map.119 = (f32[80,256]{1,0:T(8,128)}, f32[80,256]{1,0:T(8,128)}, f32[3,16,256]{2,1,0:T(8,128)}) custom-call(s32[2,80]{1,0:T(2,128)} %pad_add_fusion.tab, f32[5,5,256,256]{3,2,1,0:T(8,128)} %bitcast.27, f32[2,256,256]{2,1,0:T(8,128)} %fac1.1, f32[1,256,256]{2,1,0:T(8,128)} %fac2.1, f32[256,256]{1,0:T(8,128)} %link.1, f32[256,256]{1,0:T(8,128)} %dinv1.1, ...), custom_call_target="tpu_custom_call" | custom-call | tf_op jit(solution)/shard_map/pallas_call | solution.py:391
  84.6 1.4 %slice_bitcast_fusion = (f32[256,16]{0,1:T(8,128)}, f32[256,16]{0,1:T(8,128)}, f32[256,16]{0,1:T(8,128)}) fusion(f32[3,16,256]{2,1,0:T(8,128)} %get-tuple-element.9), kind=kLoop, calls=%fused_computation | loop fusion | bytes 98304 | tf_op jit(solution)/shard_map/transpose | solution.py:423
  86.0 1.5 %copy.19 = f32[5,1,256,16]{2,3,1,0:T(8,128)} copy(f32[5,1,256,16]{2,3,1,0:T(8,128)} %bitcast.29) | data formatting | bytes 163840
  87.5 1.5 %copy.20 = f32[5,1,256,16]{2,3,1,0:T(8,128)} copy(f32[5,1,256,16]{2,3,1,0:T(8,128)} %bitcast.28) | data formatting | bytes 163840
  (3 shorter events, 0.0 us)

commit v2 on v1

--- a/solution.py
+++ b/solution.py
@@ -30,13 +30,13 @@
 
 def kernel(
     nr, nc, na, ns, f1, f2, width,
-    tab, inv, fac1, fac2, link, dinv1, dinv2,
-    o1, o2, o3,
-    a_v, l_v, d1_v, d2_v, lt_v,
-    pf, pg, pf2, pg2, st, cw, wh, wl, acc,
+    ids1, ids2, inv, fac1, fac2, link, dinv1, dinv2,
+    out,
+    tab_v, tab, a_v, l_v, d1_v, d2_v, lt_v,
+    pf, pg, rps, rp, st, cw, wh, wl, acc,
     hop, hopped, fb, ysum, zin, xb, frb, grb,
     st2, rb, m_v, rx, n_v, q_v, s_v, u_v, w_v,
-    ld, lds, s1, pfr, pgr, pxs, pxr, bs, br, cs, cr,
+    ld, lds, lt, s1, pfr, pgr, rs_, rr, bs, br, zxs, zxr, cs, cr,
     r1s, r1r, r2s, fbr, zs, zr, ts, tr, es, er, qs, qr, us, ur, vs, vr,
 ):
     r = lax.axis_index("row")
@@ -46,7 +46,11 @@
     nz = nr // 2
     y = c // SIDE
     x = lax.rem(c, SIDE)
+    e = lax.rem(z, 2)
     mate = z * 2 + (1 - k)
+    z_up = lax.rem(z + 1, nz) * 2 + k
+    z_down = lax.rem(z + nz - 1, nz) * 2 + k
+    lanes = pl.multiple_of(128 * e, 128)
 
     def remote(src, dst, ss, rs, row, col):
         return pltpu.make_async_remote_copy(
@@ -78,29 +82,21 @@
     lax.fori_loop(1, nr, greet_row, 0)
     lax.fori_loop(1, nc, greet_col, 0)
     row8 = pl.multiple_of(128 * k + 8 * c, 8)
-    pltpu.make_async_copy(fac1.at[:, pl.ds(row8, 8), :], pf.at[pl.ds(r * f1, f1)], pfr).start()
-    pltpu.make_async_copy(fac2.at[:, pl.ds(row8, 8), :], pg.at[pl.ds(r * f2, f2)], pgr).start()
+    pltpu.make_async_copy(fac1.at[:, pl.ds(row8, 8), pl.ds(lanes, 128)], pf.at[pl.ds(r * f1, f1)], pfr).start()
+    pltpu.make_async_copy(fac2.at[:, pl.ds(row8, 8), pl.ds(lanes, 128)], pg.at[pl.ds(r * f2, f2)], pgr).start()
     for cp in small:
         cp.start()
     for b in range(ns):
         load_a(b).start()
-    pl.semaphore_wait(barrier, nr + nc - 2)
-
-    def send_pieces(fac, buf, count, rsem):
-        def go(d, carry):
-            r2 = lax.rem(r + d, nr)
-            k2 = lax.rem(r2, 2)
-            rows = pl.multiple_of(128 * k2 + 8 * c, 8)
-            remote(
-                fac.at[:, pl.ds(rows, 8), :], buf.at[pl.ds(r * count, count)], s1, rsem, r2, c
-            ).start()
-            return carry
-
-        lax.fori_loop(1, nr, go, 0)
-
-    send_pieces(fac1, pf, f1, pfr)
-    send_pieces(fac2, pg, f2, pgr)
-
+    tile = lax.broadcasted_iota(jnp.int32, (8, 128), 1)
+    which = lax.broadcasted_iota(jnp.int32, (8, 128), 0)
+    spot = jnp.full((8, 128), -1, jnp.int32)
+    for t, ids in ((0, ids1), (1, ids2)):
+        for j in range(ids.shape[0]):
+            spot = jnp.where(jnp.logical_and(tile == ids[j], which == t), j, spot)
+    tab_v[...] = spot
+    to_smem = pltpu.make_async_copy(tab_v, tab, lt)
+    to_smem.start()
     for cp in small:
         cp.wait()
     first = jnp.where(jnp.logical_and(r == 0, c == 0), 1.0, 0.0).astype(F32)
@@ -108,10 +104,27 @@
     d1_v[...] = jnp.transpose(d1_v[...]) * first
     d2_v[...] = jnp.transpose(d2_v[...]) * first
 
+    to_smem.wait()
+    pl.semaphore_wait(barrier, nr + nc - 2)
+
+    def send_pieces(fac, buf, count, rsem):
+        def go(d, carry):
+            r2 = lax.rem(r + d, nr)
+            k2 = lax.rem(r2, 2)
+            rows = pl.multiple_of(128 * k2 + 8 * c, 8)
+            side = pl.multiple_of(128 * lax.rem(r2 // 2, 2), 128)
+            remote(
+                fac.at[:, pl.ds(rows, 8), pl.ds(side, 128)], buf.at[pl.ds(r * count, count)], s1, rsem, r2, c
+            ).start()
+            return carry
+
+        lax.fori_loop(1, nr, go, 0)
+
+    send_pieces(fac1, pf, f1, pfr)
+    send_pieces(fac2, pg, f2, pgr)
+
     take(pf, pfr)
     take(pg, pgr)
-    swap_f = remote(pf, pf2, pxs.at[0], pxr.at[0], mate, c)
-    swap_g = remote(pg, pg2, pxs.at[1], pxr.at[1], mate, c)
 
     def pack(b, carry):
         def one(c2, carry2):
@@ -124,19 +137,32 @@
             return carry2
 
         lax.fori_loop(0, nc, one, 0)
-        pltpu.make_async_copy(st.at[c, b], cw.at[b, :, k, c], br.at[b]).start()
+        pltpu.make_async_copy(st.at[c, b], cw.at[b, :, e, k, c], br.at[b]).start()
 
         def go(d, carry2):
             c2 = lax.rem(c + d, nc)
-            remote(st.at[c2, b], cw.at[b, :, k, c], bs, br.at[b], r, c2).start()
+            remote(st.at[c2, b], cw.at[b, :, e, k, c], bs, br.at[b], r, c2).start()
             return carry2
 
         lax.fori_loop(1, nc, go, 0)
         return carry
 
     lax.fori_loop(0, ns, pack, 0)
-    swap_f.start()
-    swap_g.start()
+
+    other = z + 1 - 2 * e
+    for t in range(4):
+        z2 = z if t < 2 else other
+        k2 = k if t % 2 == 0 else 1 - k
+        r2 = z2 * 2 + k2
+        for a in range(na):
+            j1 = tab[0, a * nr + r2]
+            j2 = tab[1, a * nr + r2]
+            rps[t, 0, a] = jnp.where(j1 >= 0, pf[jnp.maximum(j1, 0)], 0.0)
+            rps[t, 1, a] = jnp.where(j2 >= 0, pg[jnp.maximum(j2, 0)], 0.0)
+        if t == 0:
+            pltpu.make_async_copy(rps.at[t], rp.at[e * 2 + k], rr).start()
+        else:
+            remote(rps.at[t], rp.at[e * 2 + k], rs_, rr, r2, c).start()
 
     def ring(h):
         if h == 0:
@@ -163,12 +189,9 @@
                 part(a, h, down, 0, half), fb.at[h, 1, a, pl.ds(0, half)], r1s, fbr.at[h, 1, a], r, left
             ).start()
 
-    def exchange(b):
-        return remote(cw.at[b, :, k], cw.at[b, :, k], cs, cr.at[b], mate, c)
-
     def slot(b):
-        ff = cw[b, 0].reshape(256, 256)
-        gg = cw[b, 1].reshape(256, 256)
+        ff = jnp.concatenate([cw[b, 0, 0].reshape(256, 128), cw[b, 0, 1].reshape(256, 128)], axis=1)
+        gg = jnp.concatenate([cw[b, 1, 0].reshape(256, 128), cw[b, 1, 1].reshape(256, 128)], axis=1)
         hh = gg - dot3(ff, l_v[...])
         fh, fl = split(ff)
         hhi, hlo = split(hh)
@@ -202,17 +225,26 @@
     def slots(b, carry):
         @pl.when(b < ns)
         def _():
-            take(cw.at[b, :, k], br.at[b])
-            exchange(b).start()
-
-        @pl.when(b > 0)
+            mine = cw.at[b, :, e, k]
+            take(mine, br.at[b])
+            remote(mine, mine, cs, cr.at[b], mate, c).start()
+            remote(cw.at[b, 0, e, k], cw.at[b, 0, e, k], zxs, zxr.at[b], z_down, c).start()
+            remote(cw.at[b, 1, e, k], cw.at[b, 1, e, k], zxs, zxr.at[b], z_up, c).start()
+
+        @pl.when(jnp.logical_and(b > 0, b <= ns))
         def _():
-            take(cw.at[b - 1, :, k], cr.at[b - 1])
-            slot(b - 1)
-
-        return carry
-
-    lax.fori_loop(0, ns + 1, slots, 0)
+            got = cw.at[b - 1, :, 1 - e, k]
+            take(got, zxr.at[b - 1])
+            remote(got, got, cs, cr.at[b - 1], mate, c).start()
+
+        @pl.when(b > 1)
+        def _():
+            take(cw.at[b - 2, :, :, 1 - k], cr.at[b - 2])
+            slot(b - 2)
+
+        return carry
+
+    lax.fori_loop(0, ns + 2, slots, 0)
 
     def step_two(a, carry):
         for h in range(2):
@@ -232,19 +264,16 @@
 
     lax.fori_loop(0, na, step_two, 0)
 
-    swap_f.wait()
-    swap_g.wait()
+    take(rp, rr)
     frb[...] = jnp.zeros_like(frb)
     grb[...] = jnp.zeros_like(grb)
     xb[...] = jnp.zeros_like(xb)
     for a in range(na):
-        j1 = tab[0, a * nr + r]
-        j2 = tab[1, a * nr + r]
         for h in range(2):
             lo = a * 16 + h * 8
-            i1, i2 = jnp.maximum(j1, 0), jnp.maximum(j2, 0)
-            frb[lo:lo + 8, :] = jnp.where(j1 >= 0, jnp.where(k == h, pf[i1], pf2[i1]), 0.0)
-            grb[lo:lo + 8, :] = jnp.where(j2 >= 0, jnp.where(k == h, pg[i2], pg2[i2]), 0.0)
+            for g in range(2):
+                frb[lo:lo + 8, g * 128:g * 128 + 128] = rp[g * 2 + h, 0, a]
+                grb[lo:lo + 8, g * 128:g * 128 + 128] = rp[g * 2 + h, 1, a]
 
     def second(a, carry):
         for h in range(2):
@@ -270,6 +299,17 @@
         return carry
 
     lax.fori_loop(0, na, gather, 0)
+
+    x1 = xb[:, 0:256]
+    x2 = xb[:, 256:512]
+    d1t = dot3(jnp.transpose(x1), frb[...]) + d1_v[...]
+    m_v[0] = d1t.reshape(nc, 2, 8, 256)
+    jt = dot3(lt_v[...], d1t) - dot3(jnp.transpose(grb[...]), x1)
+    m_v[1] = jt.reshape(nc, 2, 8, 256)
+    et = dot3(jnp.transpose(x2), grb[...]) + dot3(jt, l_v[...]) + d2_v[...]
+    m_v[2] = et.reshape(nc, 2, 8, 256)
+    fold = remote(m_v.at[:, :, 1 - k], rx, es, er, mate, c)
+    fold.start()
 
     lane = lax.broadcasted_iota(jnp.int32, (16, 128), 1) // 16
     for c2 in range(nc):
@@ -286,25 +326,7 @@
                         src = pltpu.roll(src, shift, axis=1)
                     val = jnp.where(lane == g, src, val)
             st2[c2, :, :, q * 128:(q + 1) * 128] = val.reshape(2, 8, 128)
-    pltpu.make_async_copy(st2.at[c], rb.at[:, c], tr).start()
-
-    def send_cols(d, carry):
-        c2 = lax.rem(c + d, nc)
-        remote(st2.at[c2], rb.at[:, c], ts, tr, r, c2).start()
-        return carry
-
-    lax.fori_loop(1, nc, send_cols, 0)
-
-    x1 = xb[:, 0:256]
-    x2 = xb[:, 256:512]
-    d1t = dot3(jnp.transpose(x1), frb[...]) + d1_v[...]
-    m_v[0] = d1t.reshape(nc, 2, 8, 256)
-    jt = dot3(lt_v[...], d1t) - dot3(jnp.transpose(grb[...]), x1)
-    m_v[1] = jt.reshape(nc, 2, 8, 256)
-    et = dot3(jnp.transpose(x2), grb[...]) + dot3(jt, l_v[...]) + d2_v[...]
-    m_v[2] = et.reshape(nc, 2, 8, 256)
-    fold = remote(m_v.at[:, :, 1 - k], rx, es, er, mate, c)
-    fold.start()
+
     take(rx, er)
     for t in range(3):
         n_v[t] = m_v[t, :, k] + rx[t]
@@ -316,15 +338,24 @@
         return carry
 
     lax.fori_loop(1, nc, send_terms, 0)
+
+    pltpu.make_async_copy(st2.at[c], rb.at[:, c], tr).start()
+
+    def send_cols(d, carry):
+        c2 = lax.rem(c + d, nc)
+        remote(st2.at[c2], rb.at[:, c], ts, tr, r, c2).start()
+        return carry
+
+    lax.fori_loop(1, nc, send_cols, 0)
 
     take(rb, tr)
     cols = jnp.transpose(rb[...].reshape(256, width))
     for a in range(na):
         j1 = tab[0, a * nr + r]
         j2 = tab[1, a * nr + r]
-        o1[a * 16:(a + 1) * 16, :] = jnp.where(j1 >= 0, -cols[a * 16:(a + 1) * 16, :], 0.0)
+        out[a * 16:(a + 1) * 16, :] = jnp.where(j1 >= 0, -cols[a * 16:(a + 1) * 16, :], 0.0)
         lo = (na + a) * 16
-        o2[a * 16:(a + 1) * 16, :] = jnp.where(j2 >= 0, -cols[lo:lo + 16, :], 0.0)
+        out[lo:lo + 16, :] = jnp.where(j2 >= 0, -cols[lo:lo + 16, :], 0.0)
 
     take(q_v, qr)
     tot = q_v[0]
@@ -349,14 +380,17 @@
     last.start()
     take(w_v.at[k], vr)
     for h in range(2):
-        o3[0, h * 8:(h + 1) * 8] = w_v[h, 0]
-        o3[1, h * 8:(h + 1) * 8] = -w_v[h, 1]
-        o3[2, h * 8:(h + 1) * 8] = w_v[h, 2]
+        lo = na * 32 + h * 8
+        out[lo:lo + 8, :] = w_v[h, 0]
+        out[lo + 16:lo + 24, :] = -w_v[h, 1]
+        out[lo + 32:lo + 40, :] = w_v[h, 2]
 
     take(pf.at[pl.ds(0, (nr - 1) * f1)], s1)
     take(pg.at[pl.ds(0, (nr - 1) * f2)], s1)
     take(st.at[pl.ds(0, nc - 1)], bs)
-    take(cw.at[:, :, 0], cs)
+    take(cw.at[:, :, :, 0], cs)
+    take(cw.at[:, :, 0, 0], zxs)
+    take(rp.at[pl.ds(0, 3)], rs_)
     take(fb, r1s)
     take(hop, r2s)
     take(zin, zs)
@@ -373,34 +407,23 @@
     nc = lax.axis_size("col")
     na, _, ns, _, ext, _ = inverse.shape
     f1, f2 = factor_first.shape[0], factor_second.shape[0]
-    tiles = max(na * nr, ns * nc)
-    ids = jnp.arange(tiles, dtype=jnp.int32)
-
-    def where_is(ids_of):
-        n = ids_of.shape[0]
-        spot = jnp.arange(1, n + 1, dtype=jnp.int32)
-        return jnp.sum(jnp.where(ids[:, None] == ids_of[None, :], spot[None, :], 0), axis=1) - 1
-
-    tab = jnp.stack([where_is(struct_first), where_is(struct_second)])
     width = -(-2 * na * 16 // 128) * 128
     deep = -(-na * 16 // 128) * 128
     any_spec = pl.BlockSpec(memory_space=pl.ANY)
     vm = lambda *s: pltpu.VMEM(s, F32)
     dma = pltpu.SemaphoreType.DMA
     half = SIDE // 2
-    o1, o2, o3 = pl.pallas_call(
+    rows = na * 16
+    o = pl.pallas_call(
         functools.partial(kernel, nr, nc, na, ns, f1, f2, width),
-        out_shape=(
-            jax.ShapeDtypeStruct((na * 16, 256), F32),
-            jax.ShapeDtypeStruct((na * 16, 256), F32),
-            jax.ShapeDtypeStruct((3, 16, 256), F32),
-        ),
-        in_specs=[pl.BlockSpec(memory_space=pltpu.SMEM)] + [any_spec] * 6,
-        out_specs=(pl.BlockSpec(memory_space=pltpu.VMEM),) * 3,
+        out_shape=jax.ShapeDtypeStruct((2 * rows + 48, 256), F32),
+        in_specs=[pl.BlockSpec(memory_space=pltpu.SMEM)] * 2 + [any_spec] * 6,
+        out_specs=pl.BlockSpec(memory_space=pltpu.VMEM),
         scratch_shapes=[
+            pltpu.VMEM((8, 128), jnp.int32), pltpu.SMEM((8, 128), jnp.int32),
             vm(na, ns, 256, 256), vm(256, 256), vm(256, 256), vm(256, 256), vm(256, 256),
-            vm(nr * f1, 8, 256), vm(nr * f2, 8, 256), vm(nr * f1, 8, 256), vm(nr * f2, 8, 256),
-            vm(nc, ns, 2, 8, 256), vm(ns, 2, 2, nc, 8, 256),
+            vm(nr * f1, 8, 128), vm(nr * f2, 8, 128), vm(4, 2, na, 8, 128), vm(4, 2, na, 8, 128),
+            vm(nc, ns, 2, 8, 128), vm(ns, 2, 2, 2, nc, 8, 128),
             pltpu.VMEM((256, 512), BF16), pltpu.VMEM((256, 512), BF16),
             vm(na, 2, SIDE, SIDE, 8, 512),
             vm(2, 2, na, half, 8, 512), vm(2, 2, na, half, 8, 512),
@@ -410,17 +433,17 @@
             vm(nc, 2, 8, width), vm(2, nc, 8, width),
             vm(3, nc, 2, 8, 256), vm(3, nc, 8, 256), vm(3, nc, 8, 256), vm(nc, 3, 8, 256),
             vm(3, 8, 256), vm(nr // 2, 3, 8, 256), vm(2, 3, 8, 256),
-            dma((ns,)), dma((3,)), dma, dma, dma, dma((2,)), dma((2,)), dma, dma((ns,)), dma, dma((ns,)),
+            dma((ns,)), dma((3,)), dma, dma, dma, dma, dma, dma, dma, dma((ns,)), dma, dma((ns,)), dma, dma((ns,)),
             dma, dma((2, 2, na)), dma, dma((2, 2, na)), dma, dma((2, na)),
             dma, dma, dma, dma, dma, dma, dma, dma, dma, dma,
         ],
         compiler_params=pltpu.CompilerParams(
             collective_id=0, has_side_effects=True, vmem_limit_bytes=56 * 1024 * 1024
         ),
-    )(tab, inverse.reshape(na, ns, ext, ext), factor_first, factor_second, link_factor, dinv_first, dinv_second)
-    panel = lambda o: jnp.swapaxes(o.reshape(na, 1, 16, 256), 2, 3)
-    turn = jnp.swapaxes
-    return (panel(o1), turn(o3[0], 0, 1), panel(o2), turn(o3[1], 0, 1), turn(o3[2], 0, 1))
+    )(struct_first, struct_second, inverse.reshape(na, ns, ext, ext), factor_first, factor_second, link_factor, dinv_first, dinv_second)
+    panel = lambda v: jnp.swapaxes(v.reshape(na, 1, 16, 256), 2, 3)
+    turn = lambda n: jnp.swapaxes(o[2 * rows + 16 * n:2 * rows + 16 * n + 16], 0, 1)
+    return (panel(o[:rows]), turn(0), panel(o[rows:2 * rows]), turn(1), turn(2))
 
 
 def solution(mesh):

time: 89.3 us -> 86.8 us (0.972)
  other arithmetic: 2.08 us -> 0 us
  local copies, waits for them, and re-layouts: 4.42 us -> 2.97 us
  Pallas kernels: 81.9 us -> 82.9 us
    unnamed x2 -> x0, local copies, waits for them, and re-layouts: 3.05 us -> none
    slice x0 -> x1, local copies, waits for them, and re-layouts: none -> 1.59 us  [body(): return (panel(o[:rows]), turn(0), panel(o[rows:2 * rows]), turn(1), turn(2))]
    reduce_sum x2 -> x0, other arithmetic: 1.49 us -> none  [where_is(): jnp.sum(jnp.where(ids[:, None] == ids_of[None, :], spot[None, :], 0), axi...]
    pallas_call x1, Pallas kernels: 81.9 us -> 82.9 us  [body(): pl.pallas_call(functools.partial(kernel, nr, nc, na, ns, f1, f2, width),...]
where the time goes in v2:
time: 86.8 us; the launch traced here: 86.5 us
  Pallas kernels  82.9 us (96%)
  local copies, waits for them, and re-layouts  2.97 us (3%)
    pallas_call x1, Pallas kernels, body(): pl.pallas_call(functools.partial(kernel, nr, nc, na, ns, f1, f2, width),...  82.9 us

profile of v2, /device:TPU:1, one launch (start us, length us, event | category | flops | bytes accessed | tf_op | source)
XLA Modules:
  0.0 86.5 jit_solution(4169940849127240800)
XLA Ops:
  0.6 82.9 %shard_map.119 = f32[208,256]{1,0:T(8,128)} custom-call(s32[32]{0:T(128)} %ids1.1, s32[16]{0:T(128)} %ids2.1, f32[5,5,256,256]{3,2,1,0:T(8,128)} %bitcast.17, f32[2,256,256]{2,1,0:T(8,128)} %fac1.1, f32[1,256,256]{2,1,0:T(8,128)} %fac2.1, f32[256,256]{1,0:T(8,128)} %link.1, f32[256,256]{1,0:T(8,128)} %dinv1.1, f32[256,256]{1,0:T(8,128)} %dinv2.1), custom_call_target="tpu_custom_call" | custom-call | tf_op jit(solution)/shard_map/pallas_call | solution.py:417
  83.6 1.4 %slice_bitcast_fusion = (f32[256,16]{0,1:T(8,128)}, f32[256,16]{0,1:T(8,128)}, f32[256,16]{0,1:T(8,128)}) fusion(f32[208,256]{1,0:T(8,128)} %shard_map.119), kind=kLoop, calls=%fused_computation | loop fusion | bytes 98304 | tf_op jit(solution)/shard_map/transpose | solution.py:445
  85.0 1.6 %fusion = (f32[80,256]{1,0:T(8,128)}, f32[80,256]{1,0:T(8,128)}) fusion(f32[208,256]{1,0:T(8,128)} %shard_map.119), kind=kLoop, calls=%fused_computation.3 | loop fusion | bytes 327680 | tf_op jit(solution)/shard_map/slice | solution.py:446

commit v3 on v2

v3 whole, which is shorter than its diff:
```python
import functools

import jax
import jax.numpy as jnp
from jax import lax
from jax.experimental import pallas as pl
from jax.experimental.pallas import tpu as pltpu
from jax.sharding import PartitionSpec as P

MESH = pl.DeviceIdType.MESH
SIDE = 4
F32 = jnp.float32
BF16 = jnp.bfloat16


def split(v):
    hi = v.astype(BF16)
    return hi, (v - hi.astype(F32)).astype(BF16)


def mm(p, q):
    return jnp.dot(p, q, preferred_element_type=F32)


def dot3(p, q):
    ph, plo = split(p)
    qh, qlo = split(q)
    return mm(ph, qh) + (mm(ph, qlo) + mm(plo, qh))


def kernel(
    nr, nc, na, ns, f1, f2, n1, n2, width,
    ids1, ids2, inv, fac1, fac2, link, dinv1, dinv2,
    out,
    tab_v, tab, a_v, l_v, d1_v, d2_v, lt_v,
    pf, pg, rps, rp, st, cw1, cw2, w3, acc,
    hop, hopped, fb, ysum, zin, x1b, x2b, frb, grb,
    st2, rb, m_v, rx, n_v, q_v, s_v, u_v, w_v,
    ld, lds, lt, s1, pfr, pgr, rs_, rr, bs, br, zxs, zxr, cs, cr,
    r1s, r1r, r2s, fbr, zs, zr, ts, tr, es, er, qs, qr, us, ur, vs, vr,
):
    r = lax.axis_index("row")
    c = lax.axis_index("col")
    k = lax.rem(r, 2)
    z = r // 2
    nz = nr // 2
    y = c // SIDE
    x = lax.rem(c, SIDE)
    e = lax.rem(z, 2)
    mate = z * 2 + (1 - k)
    z_up = lax.rem(z + 1, nz) * 2 + k
    z_down = lax.rem(z + nz - 1, nz) * 2 + k
    lanes = pl.multiple_of(128 * e, 128)
    nu = n1 + n2
    row1, row2, rowi, rowp, rowq = 0, 8, 16, 24, 25

    def remote(src, dst, ss, rs, row, col):
        return pltpu.make_async_remote_copy(
            src_ref=src, dst_ref=dst, send_sem=ss, recv_sem=rs,
            device_id=(row, col), device_id_type=MESH,
        )

    def take(ref, sem):
        pltpu.make_async_copy(ref, ref, sem).wait()

    def load_a(b):
        return pltpu.make_async_copy(inv.at[:, b], a_v.at[:, b], ld.at[b])

    small = [
        pltpu.make_async_copy(link, l_v, lds.at[0]),
        pltpu.make_async_copy(dinv1, d1_v, lds.at[1]),
        pltpu.make_async_copy(dinv2, d2_v, lds.at[2]),
    ]
    barrier = pltpu.get_barrier_semaphore()

    def greet_row(d, carry):
        pl.semaphore_signal(barrier, inc=1, device_id=(lax.rem(r + d, nr), c), device_id_type=MESH)
        return carry

    def greet_col(d, carry):
        pl.semaphore_signal(barrier, inc=1, device_id=(r, lax.rem(c + d, nc)), device_id_type=MESH)
        return carry

    lax.fori_loop(1, nr, greet_row, 0)
    lax.fori_loop(1, nc, greet_col, 0)
    row8 = pl.multiple_of(128 * k + 8 * c, 8)
    pltpu.make_async_copy(fac1.at[:, pl.ds(row8, 8), pl.ds(lanes, 128)], pf.at[pl.ds(r * f1, f1)], pfr).start()
    pltpu.make_async_copy(fac2.at[:, pl.ds(row8, 8), pl.ds(lanes, 128)], pg.at[pl.ds(r * f2, f2)], pgr).start()
    for cp in small:
        cp.start()
    for b in range(ns):
        load_a(b).start()
    pl.semaphore_wait(barrier, nr + nc - 2)

    def send_pieces(fac, buf, count, rsem):
        def go(d, carry):
            r2 = lax.rem(r + d, nr)
            k2 = lax.rem(r2, 2)
            rows = pl.multiple_of(128 * k2 + 8 * c, 8)
            side = pl.multiple_of(128 * lax.rem(r2 // 2, 2), 128)
            remote(
                fac.at[:, pl.ds(rows, 8), pl.ds(side, 128)], buf.at[pl.ds(r * count, count)], s1, rsem, r2, c
            ).start()
            return carry

        lax.fori_loop(1, nr, go, 0)

    send_pieces(fac1, pf, f1, pfr)
    send_pieces(fac2, pg, f2, pgr)

    tile = lax.broadcasted_iota(jnp.int32, (8, 128), 1)
    at1 = jnp.zeros((8, 128), jnp.int32)
    at2 = jnp.zeros((8, 128), jnp.int32)
    for j in range(ids1.shape[0]):
        at1 = jnp.where(tile == ids1[j], j + 1, at1)
    for j in range(ids2.shape[0]):
        at2 = jnp.where(tile == ids2[j], j + 1, at2)
    in2 = jnp.where(at2 > 0, 1, 0)
    only1 = jnp.where(at1 > 0, 1, 0) - in2

    def lower(v):
        tot = jnp.zeros_like(v)
        for d in range(1, na):
            tot = tot + jnp.where(tile >= d * nc, pltpu.roll(v, d * nc, axis=1), 0)
        return tot

    def fold_tiles(v):
        tot = v
        for d in range(1, na):
            tot = tot + pltpu.roll(v, 128 - d * nc, axis=1)
        return tot

    def spread(v):
        tot = v
        for d in range(1, na):
            tot = tot + jnp.where(tile >= d * nc, pltpu.roll(v, d * nc, axis=1), 0)
        return tot

    count2 = spread(jnp.where(tile < nc, fold_tiles(in2), 0))
    rank = jnp.where(in2 > 0, lower(in2), count2 + lower(only1))
    line = lax.broadcasted_iota(jnp.int32, (8, 128), 0)
    t1 = jnp.zeros((8, 128), jnp.int32)
    t2 = jnp.zeros((8, 128), jnp.int32)
    ti = jnp.zeros((8, 128), jnp.int32)
    for a in range(n1):
        hit = jnp.logical_and(at1 > 0, rank == a)
        t1 = jnp.where(line == a, fold_tiles(jnp.where(hit, at1, 0)), t1)
        t2 = jnp.where(line == a, fold_tiles(jnp.where(hit, at2, 0)), t2)
        ti = jnp.where(line == a, fold_tiles(jnp.where(hit, tile // nc, 0)), ti)
    tab_v[0:8, :] = t1 - 1
    tab_v[8:16, :] = t2 - 1
    tab_v[16:24, :] = ti
    tab_v[24:32, :] = jnp.where(
        line == 0, jnp.where(at1 > 0, rank, -1), jnp.where(in2 > 0, rank, -1)
    )
    to_smem = pltpu.make_async_copy(tab_v, tab, lt)
    to_smem.start()
    for cp in small:
        cp.wait()
    first = jnp.where(jnp.logical_and(r == 0, c == 0), 1.0, 0.0).astype(F32)
    lt_v[...] = jnp.transpose(l_v[...])
    d1_v[...] = jnp.transpose(d1_v[...]) * first
    d2_v[...] = jnp.transpose(d2_v[...]) * first

    to_smem.wait()
    take(pf, pfr)
    take(pg, pgr)

    def pack(b, carry):
        def send(fg, cw):
            def one(c2, carry2):
                j = tab[(row1, row2)[fg] + b, c2]
                v = (pf, pg)[fg][jnp.maximum(j, 0)]
                st[fg, b, c2] = jnp.where(j >= 0, v, 0.0)
                return carry2

            lax.fori_loop(0, nc, one, 0)
            pltpu.make_async_copy(st.at[fg, b, c], cw.at[b, e, k, c], br.at[fg, b]).start()

            def go(d, carry2):
                c2 = lax.rem(c + d, nc)
                remote(st.at[fg, b, c2], cw.at[b, e, k, c], bs.at[fg], br.at[fg, b], r, c2).start()
                return carry2

            lax.fori_loop(1, nc, go, 0)

        send(0, cw1)

        @pl.when(b < n2)
        def _():
            send(1, cw2)

        return carry

    lax.fori_loop(0, n1, pack, 0)

    other = z + 1 - 2 * e
    for t in range(4):
        z2 = z if t < 2 else other
        k2 = k if t % 2 == 0 else 1 - k
        r2 = z2 * 2 + k2
        for a in range(n1):
            j1 = tab[row1 + a, r2]
            rps[t, a] = jnp.where(j1 >= 0, pf[jnp.maximum(j1, 0)], 0.0)
        for a in range(n2):
            j2 = tab[row2 + a, r2]
            rps[t, n1 + a] = jnp.where(j2 >= 0, pg[jnp.maximum(j2, 0)], 0.0)
        if t == 0:
            pltpu.make_async_copy(rps.at[t], rp.at[e * 2 + k], rr).start()
        else:
            remote(rps.at[t], rp.at[e * 2 + k], rs_, rr, r2, c).start()

    def ring(h):
        if h == 0:
            return x, y * SIDE + lax.rem(x + 1, SIDE), y * SIDE + lax.rem(x + SIDE - 1, SIDE)
        return y, lax.rem(y + 1, SIDE) * SIDE + x, lax.rem(y + SIDE - 1, SIDE) * SIDE + x

    half = SIDE // 2

    def part(a, h, who, lo, n):
        if h == 0:
            return acc.at[a, 0, pl.ds(lo, n), who]
        return acc.at[a, 1, who, pl.ds(lo, n)]

    def step_one(a):
        for h in range(2):
            u, right, left = ring(h)
            up, down, far = lax.rem(u + 1, SIDE), lax.rem(u + SIDE - 1, SIDE), lax.rem(u + 2, SIDE)
            remote(part(a, h, far, 0, half), hop.at[h, 0, a], r1s, r1r.at[h, 0, a], r, right).start()
            remote(part(a, h, far, half, half), hop.at[h, 1, a], r1s, r1r.at[h, 1, a], r, left).start()
            remote(
                part(a, h, up, half, half), fb.at[h, 0, a, pl.ds(half, half)], r1s, fbr.at[h, 0, a], r, right
            ).start()
            remote(
                part(a, h, down, 0, half), fb.at[h, 1, a, pl.ds(0, half)], r1s, fbr.at[h, 1, a], r, left
            ).start()

    def whole(cw, b):
        return jnp.concatenate([cw[b, 0].reshape(256, 128), cw[b, 1].reshape(256, 128)], axis=1)

    def slot(b):
        ff = whole(cw1, b)
        fh, fl = split(ff)
        w3[0:256, 0:256] = fh
        w3[256:512, 0:256] = fl
        w3[512:768, 0:256] = fh
        fll = dot3(ff, l_v[...])

        def put(hh):
            hhi, hlo = split(hh)
            w3[0:256, 256:512] = hhi
            w3[256:512, 256:512] = hlo
            w3[512:768, 256:512] = hhi

        @pl.when(b < n2)
        def _():
            put(whole(cw2, jnp.minimum(b, n2 - 1)) - fll)

        @pl.when(b >= n2)
        def _():
            put(-fll)

        col = tab[rowi + b, c]

        def rowstep(a, cols):
            ah, al = split(a_v[tab[rowi + a, r], col])
            got = mm(jnp.concatenate([ah, ah, al], axis=1), w3[:, 0:cols])
            for fg in range(cols // 256):
                u = n1 * fg + a
                g = got[:, fg * 256:fg * 256 + 256].reshape(2, SIDE, SIDE, 8, 256)

                @pl.when(b == 0)
                def _():
                    acc[u] = g

                @pl.when(b > 0)
                def _():
                    acc[u] += g

                @pl.when(b == n1 - 1)
                def _():
                    step_one(u)

        def both(a, carry):
            rowstep(a, 512)
            return carry

        def first_only(a, carry):
            rowstep(a, 256)
            return carry

        lax.fori_loop(0, n2, both, 0)
        if n2 < n1:
            lax.fori_loop(n2, n1, first_only, 0)

    def swap(cw, fg, b):
        mine = cw.at[b, e, k]
        take(mine, br.at[fg, b])
        remote(mine, mine, cs.at[fg], cr.at[fg, b], mate, c).start()
        remote(mine, mine, zxs.at[fg], zxr.at[fg, b], (z_down, z_up)[fg], c).start()

    def hand(cw, fg, b):
        got = cw.at[b, 1 - e, k]
        take(got, zxr.at[fg, b])
        remote(got, got, cs.at[fg], cr.at[fg, b], mate, c).start()

    def slots(b, carry):
        @pl.when(b < n1)
        def _():
            swap(cw1, 0, b)

        @pl.when(b < n2)
        def _():
            swap(cw2, 1, b)

        @pl.when(jnp.logical_and(b > 0, b <= n1))
        def _():
            hand(cw1, 0, b - 1)

        @pl.when(jnp.logical_and(b > 0, b <= n2))
        def _():
            hand(cw2, 1, b - 1)

        @pl.when(b > 1)
        def _():
            take(cw1.at[b - 2, :, 1 - k], cr.at[0, b - 2])

            @pl.when(b - 2 < n2)
            def _():
                take(cw2.at[b - 2, :, 1 - k], cr.at[1, b - 2])

            slot(b - 2)

        return carry

    for b in range(ns):
        load_a(b).wait()
    lax.fori_loop(0, n1 + 2, slots, 0)

    def step_two(a, carry):
        for h in range(2):
            u, right, left = ring(h)
            up, down = lax.rem(u + 1, SIDE), lax.rem(u + SIDE - 1, SIDE)
            take(hop.at[h, 0, a], r1r.at[h, 0, a])
            hopped[h, 0, a] = hop[h, 0, a] + part(a, h, up, 0, half)[...]
            remote(
                hopped.at[h, 0, a], fb.at[h, 0, a, pl.ds(0, half)], r2s, fbr.at[h, 0, a], r, right
            ).start()
            take(hop.at[h, 1, a], r1r.at[h, 1, a])
            hopped[h, 1, a] = hop[h, 1, a] + part(a, h, down, half, half)[...]
            remote(
                hopped.at[h, 1, a], fb.at[h, 1, a, pl.ds(half, half)], r2s, fbr.at[h, 1, a], r, left
            ).start()
        return carry

    lax.fori_loop(0, nu, step_two, 0)

    take(rp, rr)
    frb[...] = jnp.zeros_like(frb)
    grb[...] = jnp.zeros_like(grb)
    x1b[...] = jnp.zeros_like(x1b)
    x2b[...] = jnp.zeros_like(x2b)
    for h in range(2):
        for g in range(2):
            for a in range(n1):
                frb[a * 16 + h * 8:a * 16 + h * 8 + 8, g * 128:g * 128 + 128] = rp[g * 2 + h, a]
            for a in range(n2):
                grb[a * 16 + h * 8:a * 16 + h * 8 + 8, g * 128:g * 128 + 128] = rp[g * 2 + h, n1 + a]

    def second(a, carry):
        for h in range(2):
            u = ring(h)[0]
            take(fb.at[h, 0, a], fbr.at[h, 0, a])
            take(fb.at[h, 1, a], fbr.at[h, 1, a])
            ysum[h, a] = part(a, h, u, 0, SIDE)[...] + (fb[h, 0, a] + fb[h, 1, a])
            v = y if h == 0 else x
            for d in range(1, SIDE):
                v2 = lax.rem(v + d, SIDE)
                col = v2 * SIDE + x if h == 0 else y * SIDE + v2
                remote(ysum.at[h, a, v2], zin.at[h, a, d - 1], zs, zr.at[h, a], r, col).start()
        return carry

    lax.fori_loop(0, nu, second, 0)

    def gather(fg, buf):
        def one(a, carry):
            u = n1 * fg + a
            for h in range(2):
                v = y if h == 0 else x
                take(zin.at[h, u], zr.at[h, u])
                tot = ysum[h, u, v] + (zin[h, u, 0] + zin[h, u, 1] + zin[h, u, 2])
                buf[pl.ds(pl.multiple_of(a * 16 + h * 8, 8), 8), :] = tot
            return carry

        lax.fori_loop(0, (n1, n2)[fg], one, 0)

    gather(0, x1b)
    x1 = x1b[...]
    d1t = dot3(jnp.transpose(x1), frb[...]) + d1_v[...]
    m_v[0] = d1t.reshape(nc, 2, 8, 256)
    jt = dot3(lt_v[...], d1t) - dot3(jnp.transpose(grb[...]), x1)
    m_v[1] = jt.reshape(nc, 2, 8, 256)

    def fold(t):
        return remote(m_v.at[t, :, 1 - k], rx.at[t], es, er.at[t], mate, c)

    fold(0).start()
    fold(1).start()
    base = dot3(jt, l_v[...]) + d2_v[...]
    gather(1, x2b)
    et = dot3(jnp.transpose(x2b[...]), grb[...]) + base
    m_v[2] = et.reshape(nc, 2, 8, 256)
    fold(2).start()

    def send_term(t):
        take(rx.at[t], er.at[t])
        n_v[t] = m_v[t, :, k] + rx[t]
        pltpu.make_async_copy(n_v.at[t, c], q_v.at[t, c], qr.at[t]).start()

        def go(d, carry):
            c2 = lax.rem(c + d, nc)
            remote(n_v.at[t, c2], q_v.at[t, c], qs, qr.at[t], r, c2).start()
            return carry

        lax.fori_loop(1, nc, go, 0)

    for t in range(3):
        send_term(t)

    lane = lax.broadcasted_iota(jnp.int32, (16, 128), 1) // 16
    for c2 in range(nc):
        blk, off = c2 // 8, c2 % 8
        for q in range(width // 128):
            val = jnp.zeros((16, 128), F32)
            for g in range(8):
                u = q * 8 + g
                if u < nu:
                    buf, a = (x1b, u) if u < n1 else (x2b, u - n1)
                    src = buf[a * 16:a * 16 + 16, blk * 128:blk * 128 + 128]
                    shift = (16 * (g - off)) % 128
                    if shift:
                        src = pltpu.roll(src, shift, axis=1)
                    val = jnp.where(lane == g, src, val)
            st2[c2, :, :, q * 128:(q + 1) * 128] = val.reshape(2, 8, 128)
    pltpu.make_async_copy(st2.at[c], rb.at[:, c], tr).start()

    def send_cols(d, carry):
        c2 = lax.rem(c + d, nc)
        remote(st2.at[c2], rb.at[:, c], ts, tr, r, c2).start()
        return carry

    lax.fori_loop(1, nc, send_cols, 0)

    def send_sum(t):
        take(q_v.at[t], qr.at[t])
        tot = q_v[t, 0]
        for i in range(1, nc):
            tot = tot + q_v[t, i]
        s_v[t] = tot
        pltpu.make_async_copy(s_v.at[t], u_v.at[t, z], ur.at[t]).start()

        def go(d, carry):
            z2 = lax.rem(z + d, nz)
            remote(s_v.at[t], u_v.at[t, z], us, ur.at[t], z2 * 2 + k, c).start()
            return carry

        lax.fori_loop(1, nz, go, 0)

    for t in range(3):
        send_sum(t)

    take(rb, tr)
    cols = jnp.transpose(rb[...].reshape(256, width))
    for fg in range(2):
        for a in range(na):
            slot_of = tab[(rowp, rowq)[fg], a * nr + r]
            val = jnp.zeros((16, 256), F32)
            for i in range((n1, n2)[fg]):
                lo = (n1 * fg + i) * 16
                val = jnp.where(slot_of == i, -cols[lo:lo + 16, :], val)
            lo = (na * fg + a) * 16
            out[lo:lo + 16, :] = val

    for t in range(3):
        take(u_v.at[t], ur.at[t])
        tot = u_v[t, 0]
        for i in range(1, nz):
            tot = tot + u_v[t, i]
        w_v[k, t] = tot
    last = remote(w_v.at[k], w_v.at[k], vs, vr, mate, c)
    last.start()
    take(w_v.at[k], vr)
    for h in range(2):
        lo = na * 32 + h * 8
        out[lo:lo + 8, :] = w_v[h, 0]
        out[lo + 16:lo + 24, :] = -w_v[h, 1]
        out[lo + 32:lo + 40, :] = w_v[h, 2]

    take(pf.at[pl.ds(0, (nr - 1) * f1)], s1)
    take(pg.at[pl.ds(0, (nr - 1) * f2)], s1)
    for fg, cw, n in ((0, cw1, n1), (1, cw2, n2)):
        take(st.at[fg, pl.ds(0, n), pl.ds(0, nc - 1)], bs.at[fg])
        take(cw.at[:, :, 0], cs.at[fg])
        take(cw.at[:, 0, 0], zxs.at[fg])
    take(rp.at[pl.ds(0, 3)], rs_)
    take(fb, r1s)
    take(hop, r2s)
    take(zin, zs)
    take(rb.at[:, pl.ds(0, nc - 1)], ts)
    take(rx, es)
    take(q_v.at[:, pl.ds(0, nc - 1)], qs)
    take(u_v.at[:, pl.ds(0, nz - 1)], us)
    take(w_v.at[0], vs)


def part_out(rows, o, p1, p2, g1, g2, g3):
    p1[...] = o[0:rows, :]
    p2[...] = o[rows:2 * rows, :]
    for n, g in enumerate((g1, g2, g3)):
        g[...] = o[2 * rows + 16 * n:2 * rows + 16 * n + 16, :]


def fused(n1, n2, ident, struct_first, struct_second, inverse, factor_first, factor_second, link_factor, dinv_first, dinv_second):
    nr = lax.axis_size("row")
    nc = lax.axis_size("col")
    na, ns, ext, _ = inverse.shape
    f1, f2 = factor_first.shape[0], factor_second.shape[0]
    assert nr == nc == SIDE * SIDE and na == ns and na * nc <= 128 and n1 <= 8
    nu = n1 + n2
    nz = nr // 2
    width = -(-nu * 16 // 128) * 128
    deep = -(-n1 * 16 // 128) * 128
    rows = na * 16
    any_spec = pl.BlockSpec(memory_space=pl.ANY)
    vm = lambda *s: pltpu.VMEM(s, F32)
    dma = pltpu.SemaphoreType.DMA
    half = SIDE // 2
    return pl.pallas_call(
        functools.partial(kernel, nr, nc, na, ns, f1, f2, n1, n2, width),
        out_shape=jax.ShapeDtypeStruct((2 * rows + 48, 256), F32),
        in_specs=[pl.BlockSpec(memory_space=pltpu.SMEM)] * 2 + [any_spec] * 6,
        out_specs=pl.BlockSpec(memory_space=pltpu.VMEM),
        scratch_shapes=[
            pltpu.VMEM((32, 128), jnp.int32), pltpu.SMEM((32, 128), jnp.int32),
            vm(na, ns, 256, 256), vm(256, 256), vm(256, 256), vm(256, 256), vm(256, 256),
            vm(nr * f1, 8, 128), vm(nr * f2, 8, 128), vm(4, nu, 8, 128), vm(4, nu, 8, 128),
            vm(2, n1, nc, 8, 128), vm(n1, 2, 2, nc, 8, 128), vm(n2, 2, 2, nc, 8, 128),
            pltpu.VMEM((768, 512), BF16),
            vm(nu, 2, SIDE, SIDE, 8, 256),
            vm(2, 2, nu, half, 8, 256), vm(2, 2, nu, half, 8, 256),
            vm(2, 2, nu, SIDE, 8, 256), vm(2, nu, SIDE, 8, 256),
            vm(2, nu, SIDE - 1, 8, 256),
            vm(deep, 256), vm(deep, 256), vm(deep, 256), vm(deep, 256),
            vm(nc, 2, 8, width), vm(2, nc, 8, width),
            vm(3, nc, 2, 8, 256), vm(3, nc, 8, 256), vm(3, nc, 8, 256), vm(3, nc, 8, 256),
            vm(3, 8, 256), vm(3, nz, 8, 256), vm(2, 3, 8, 256),
            dma((ns,)), dma((3,)), dma, dma, dma, dma, dma, dma,
            dma((2,)), dma((2, n1)), dma((2,)), dma((2, n1)), dma((2,)), dma((2, n1)),
            dma, dma((2, 2, nu)), dma, dma((2, 2, nu)), dma, dma((2, nu)),
            dma, dma, dma, dma((3,)), dma, dma((3,)), dma, dma((3,)), dma, dma,
        ],
        compiler_params=pltpu.CompilerParams(
            collective_id=ident, has_side_effects=True, vmem_limit_bytes=56 * 1024 * 1024
        ),
    )(struct_first, struct_second, inverse, factor_first, factor_second, link_factor, dinv_first, dinv_second)


def body(inverse, struct_first, struct_second, factor_first, factor_second, link_factor, dinv_first, dinv_second):
    na, _, ns, _, ext, _ = inverse.shape
    rows = na * 16
    args = (
        struct_first, struct_second, inverse.reshape(na, ns, ext, ext),
        factor_first, factor_second, link_factor, dinv_first, dinv_second,
    )
    o = fused(na, na, 0, *args)
    small = jax.ShapeDtypeStruct((16, 256), F32)
    tall = jax.ShapeDtypeStruct((rows, 256), F32)
    p1, p2, g1, g2, g3 = pl.pallas_call(
        functools.partial(part_out, rows),
        out_shape=(tall, tall, small, small, small),
    )(o)
    panel = lambda v: jnp.swapaxes(v.reshape(na, 1, 16, 256), 2, 3)
    turn = lambda v: jnp.swapaxes(v, 0, 1)
    return (panel(p1), turn(g1), panel(p2), turn(g2), turn(g3))


def solution(mesh):
    placed = (
        P(None, "row", None, "col", None, None),
        P(),
        P(),
        P("row", None, None),
        P("row", None, None),
        P(),
        P(),
        P(),
    )
    return jax.shard_map(
        body,
        mesh=mesh,
        in_specs=placed,
        out_specs=(
            P(None, "row", None, "col"),
            P(None, "col"),
            P(None, "row", None, "col"),
            P(None, "col"),
            P(None, "col"),
        ),
        check_vma=False,
    )
```

time: 86.8 us -> 79.4 us (0.915)
  Pallas kernels: 82.9 us -> 78.6 us
  local copies, waits for them, and re-layouts: 2.97 us -> 0 us
    pallas_call x1 -> x2, Pallas kernels: 82.9 us -> 78.6 us  [the longest x1 77 us: fused(): pl.pallas_call(functools.partial(kernel, nr, nc, na, ns, f1, f2, n1, n2,...]
    slice x1 -> x0, local copies, waits for them, and re-layouts: 1.59 us -> none  [body(): return (panel(o[:rows]), turn(0), panel(o[rows:2 * rows]), turn(1), turn(2))]
    transpose x1 -> x0, local copies, waits for them, and re-layouts: 1.37 us -> none  [body(): jnp.swapaxes(o[2 * rows + 16 * n:2 * rows + 16 * n + 16], 0, 1)]
where the time goes in v3:
time: 79.4 us; the launch traced here: 79.3 us
  Pallas kernels  78.6 us (99%)
    pallas_call x1, Pallas kernels, fused(): pl.pallas_call(functools.partial(kernel, nr, nc, na, ns, f1, f2, n1, n2,...  77 us
    pallas_call x1, Pallas kernels, body(): pl.pallas_call(functools.partial(part_out, rows), out_shape=(tall, tall,...  1.61 us

profile of v3, /device:TPU:1, one launch (start us, length us, event | category | flops | bytes accessed | tf_op | source)
XLA Modules:
  0.0 79.3 jit_solution(15907330363588123017)
XLA Ops:
  0.6 77.0 %shard_map.119.o = f32[208,256]{1,0:T(8,128)} custom-call(s32[32]{0:T(128)} %ids1.1, s32[16]{0:T(128)} %ids2.1, f32[5,5,256,256]{3,2,1,0:T(8,128)} %bitcast.14, f32[2,256,256]{2,1,0:T(8,128)} %fac1.1, f32[1,256,256]{2,1,0:T(8,128)} %fac2.1, f32[256,256]{1,0:T(8,128)} %link.1, f32[256,256]{1,0:T(8,128)} %dinv1.1, f32[256,256]{1,0:T(8,128)} %dinv2.1), custom_call_target="tpu_custom_call" | custom-call | tf_op jit(solution)/shard_map/pallas_call | solution.py:538
  77.6 1.6 %shard_map.120 = (f32[80,256]{1,0:T(8,128)}, f32[80,256]{1,0:T(8,128)}, f32[16,256]{1,0:T(8,128)}, f32[16,256]{1,0:T(8,128)}, f32[16,256]{1,0:T(8,128)}) custom-call(f32[208,256]{1,0:T(8,128)} %shard_map.119.o), custom_call_target="tpu_custom_call" | custom-call | tf_op jit(solution)/shard_map/pallas_call | solution.py:578

commit v4 on v3

--- a/solution.py
+++ b/solution.py
@@ -9,6 +9,7 @@
 
 MESH = pl.DeviceIdType.MESH
 SIDE = 4
+TIGHT = (4, 3)
 F32 = jnp.float32
 BF16 = jnp.bfloat16
 
@@ -33,7 +34,7 @@
     ids1, ids2, inv, fac1, fac2, link, dinv1, dinv2,
     out,
     tab_v, tab, a_v, l_v, d1_v, d2_v, lt_v,
-    pf, pg, rps, rp, st, cw1, cw2, w3, acc,
+    pf, pg, rps, rp, st, cw1, cw2, lhs, w3, acc,
     hop, hopped, fb, ysum, zin, x1b, x2b, frb, grb,
     st2, rb, m_v, rx, n_v, q_v, s_v, u_v, w_v,
     ld, lds, lt, s1, pfr, pgr, rs_, rr, bs, br, zxs, zxr, cs, cr,
@@ -238,19 +239,19 @@
     def whole(cw, b):
         return jnp.concatenate([cw[b, 0].reshape(256, 128), cw[b, 1].reshape(256, 128)], axis=1)
 
-    def slot(b):
+    def weights(b):
         ff = whole(cw1, b)
         fh, fl = split(ff)
-        w3[0:256, 0:256] = fh
-        w3[256:512, 0:256] = fl
-        w3[512:768, 0:256] = fh
+        w3[b, 0:256, 0:256] = fh
+        w3[b, 256:512, 0:256] = fl
+        w3[b, 512:768, 0:256] = fh
         fll = dot3(ff, l_v[...])
 
         def put(hh):
             hhi, hlo = split(hh)
-            w3[0:256, 256:512] = hhi
-            w3[256:512, 256:512] = hlo
-            w3[512:768, 256:512] = hhi
+            w3[b, 0:256, 256:512] = hhi
+            w3[b, 256:512, 256:512] = hlo
+            w3[b, 512:768, 256:512] = hhi
 
         @pl.when(b < n2)
         def _():
@@ -260,11 +261,15 @@
         def _():
             put(-fll)
 
-        col = tab[rowi + b, c]
-
+    def term(a, b, lo, cols):
+        v = lhs[b, a]
+        return mm(jnp.concatenate([v[:, 0:256], v[:, 0:256], v[:, 256:512]], axis=1), w3[b, :, lo:lo + cols])
+
+    early = n1 - 2
+
+    def part_sums(b):
         def rowstep(a, cols):
-            ah, al = split(a_v[tab[rowi + a, r], col])
-            got = mm(jnp.concatenate([ah, ah, al], axis=1), w3[:, 0:cols])
+            got = term(a, b, 0, cols)
             for fg in range(cols // 256):
                 u = n1 * fg + a
                 g = got[:, fg * 256:fg * 256 + 256].reshape(2, SIDE, SIDE, 8, 256)
@@ -277,10 +282,6 @@
                 def _():
                     acc[u] += g
 
-                @pl.when(b == n1 - 1)
-                def _():
-                    step_one(u)
-
         def both(a, carry):
             rowstep(a, 512)
             return carry
@@ -292,6 +293,15 @@
         lax.fori_loop(0, n2, both, 0)
         if n2 < n1:
             lax.fori_loop(n2, n1, first_only, 0)
+
+    def finish(fg):
+        def one(a, carry):
+            got = term(a, early, 256 * fg, 256) + term(a, early + 1, 256 * fg, 256)
+            acc[n1 * fg + a] += got.reshape(2, SIDE, SIDE, 8, 256)
+            step_one(n1 * fg + a)
+            return carry
+
+        lax.fori_loop(0, (n1, n2)[fg], one, 0)
 
     def swap(cw, fg, b):
         mine = cw.at[b, e, k]
@@ -329,13 +339,28 @@
             def _():
                 take(cw2.at[b - 2, :, 1 - k], cr.at[1, b - 2])
 
-            slot(b - 2)
+            weights(b - 2)
+
+            @pl.when(b - 2 < early)
+            def _():
+                part_sums(b - 2)
 
         return carry
 
     for b in range(ns):
         load_a(b).wait()
+
+    def cast(i, carry):
+        a, b = i // n1, lax.rem(i, n1)
+        ah, al = split(a_v[tab[rowi + a, r], tab[rowi + b, c]])
+        lhs[b, a, :, 0:256] = ah
+        lhs[b, a, :, 256:512] = al
+        return carry
+
+    lax.fori_loop(0, n1 * n1, cast, 0)
     lax.fori_loop(0, n1 + 2, slots, 0)
+    finish(0)
+    finish(1)
 
     def step_two(a, carry):
         for h in range(2):
@@ -511,6 +536,17 @@
     take(q_v.at[:, pl.ds(0, nc - 1)], qs)
     take(u_v.at[:, pl.ds(0, nz - 1)], us)
     take(w_v.at[0], vs)
+
+
+def spread_fits(n, ids1, ids2, out):
+    lane = lax.broadcasted_iota(jnp.int32, (8, 128), 1)
+    bad = jnp.zeros((8, 128), F32)
+    for ids, most in ((ids1, TIGHT[0]), (ids2, TIGHT[1])):
+        count = jnp.zeros((8, 128), F32)
+        for j in range(ids.shape[0]):
+            count = count + jnp.where(lane == lax.rem(ids[j], n), 1.0, 0.0)
+        bad = jnp.maximum(bad, count - most)
+    out[0] = jnp.where(jnp.max(bad) > 0.5, 0, 1)
 
 
 def part_out(rows, o, p1, p2, g1, g2, g3):
@@ -545,7 +581,7 @@
             vm(na, ns, 256, 256), vm(256, 256), vm(256, 256), vm(256, 256), vm(256, 256),
             vm(nr * f1, 8, 128), vm(nr * f2, 8, 128), vm(4, nu, 8, 128), vm(4, nu, 8, 128),
             vm(2, n1, nc, 8, 128), vm(n1, 2, 2, nc, 8, 128), vm(n2, 2, 2, nc, 8, 128),
-            pltpu.VMEM((768, 512), BF16),
+            pltpu.VMEM((n1, n1, 256, 512), BF16), pltpu.VMEM((n1, 768, 512), BF16),
             vm(nu, 2, SIDE, SIDE, 8, 256),
             vm(2, 2, nu, half, 8, 256), vm(2, 2, nu, half, 8, 256),
             vm(2, 2, nu, SIDE, 8, 256), vm(2, nu, SIDE, 8, 256),
@@ -572,7 +608,15 @@
         struct_first, struct_second, inverse.reshape(na, ns, ext, ext),
         factor_first, factor_second, link_factor, dinv_first, dinv_second,
     )
-    o = fused(na, na, 0, *args)
+    roomy = lambda *v: fused(na, na, 0, *v)
+    tight = lambda *v: fused(TIGHT[0], TIGHT[1], 1, *v)
+    fits = pl.pallas_call(
+        functools.partial(spread_fits, lax.axis_size("row")),
+        out_shape=jax.ShapeDtypeStruct((1,), jnp.int32),
+        in_specs=[pl.BlockSpec(memory_space=pltpu.SMEM)] * 2,
+        out_specs=pl.BlockSpec(memory_space=pltpu.SMEM),
+    )(struct_first, struct_second)
+    o = lax.cond(fits[0] > 0, tight, roomy, *args)
     small = jax.ShapeDtypeStruct((16, 256), F32)
     tall = jax.ShapeDtypeStruct((rows, 256), F32)
     p1, p2, g1, g2, g3 = pl.pallas_call(

time: 79.4 us -> 70.3 us (0.89)
  Pallas kernels: 78.6 us -> 68.9 us
    pallas_call x1, Pallas kernels: 77 us -> 66.8 us  [fused(): pl.pallas_call(functools.partial(kernel, nr, nc, na, ns, f1, f2, n1, n2,...]
    pallas_call x0 -> x1, Pallas kernels: none -> 1.39 us  [body(): pl.pallas_call(functools.partial(spread_fits, lax.axis_size('row')), out_...]
    pallas_call x1, Pallas kernels: 1.61 us -> 0.69 us  [body(): pl.pallas_call(functools.partial(part_out, rows), out_shape=(tall, tall,...]
where the time goes in v4:
time: 70.3 us; the launch traced here: 70.2 us
  Pallas kernels  68.9 us (98%)
  between operations  1.3 us (2%)
    pallas_call x1, Pallas kernels, fused(): pl.pallas_call(functools.partial(kernel, nr, nc, na, ns, f1, f2, n1, n2,...  66.8 us

profile of v4, /device:TPU:1, one launch (start us, length us, event | category | flops | bytes accessed | tf_op | source)
XLA Modules:
  0.0 70.2 jit_solution(15308757108014258052)
XLA Ops:
  0.6 1.4 %shard_map.119 = s32[1]{0:T(128)} custom-call(s32[32]{0:T(128)} %ids1.1, s32[16]{0:T(128)} %ids2.1), custom_call_target="tpu_custom_call" | custom-call | tf_op jit(solution)/shard_map/pallas_call | solution.py:613
  2.7 66.9 %conditional.1 = (f32[208,256]{1,0:T(8,128)S(1)}) conditional(s32[]{:T(128)} %bitcast, (s32[32]{0:T(128)}, s32[16]{0:T(128)}, f32[5,5,256,256]{3,2,1,0:T(8,128)}, f32[2,256,256]{2,1,0:T(8,128)}, f32[1,256,256]{2,1,0:T(8,128)}, /*index=5*/f32[256,256]{1,0:T(8,128)}, f32[256,256]{1,0:T(8,128)}, f32[256,256]{1,0:T(8,128)}) %tuple.18, (s32[32]{0:T(128)}, ...), branch_computations={%region_0.0_spmd, %region_1.0_spmd} | conditional | bytes 8 | solution.py:619
  2.7 66.8 %branch_1_fun.1 = f32[208,256]{1,0:T(8,128)S(1)} custom-call(s32[32]{0:T(128)} %get-tuple-element.43.ids1, s32[16]{0:T(128)} %get-tuple-element.44.ids2, f32[5,5,256,256]{3,2,1,0:T(8,128)} %get-tuple-element.45.inv, f32[2,256,256]{2,1,0:T(8,128)} %get-tuple-element.46.fac1, f32[1,256,256]{2,1,0:T(8,128)} %get-tuple-element.47.fac2, ...), custom_call_target="tpu_custom_call" | custom-call | tf_op jit(solution)/shard_map/cond/branch_1_fun/pallas_call | solution.py:574
  69.5 0.7 shard_map.120

commit v5 on v4

--- a/solution.py
+++ b/solution.py
@@ -10,6 +10,8 @@
 MESH = pl.DeviceIdType.MESH
 SIDE = 4
 TIGHT = (4, 3)
+HAND_LAG = 3
+USE_LAG = 5
 F32 = jnp.float32
 BF16 = jnp.bfloat16
 
@@ -34,7 +36,7 @@
     ids1, ids2, inv, fac1, fac2, link, dinv1, dinv2,
     out,
     tab_v, tab, a_v, l_v, d1_v, d2_v, lt_v,
-    pf, pg, rps, rp, st, cw1, cw2, lhs, w3, acc,
+    pf, pg, rps, rp, st, cw, lhs, w3, acc,
     hop, hopped, fb, ysum, zin, x1b, x2b, frb, grb,
     st2, rb, m_v, rx, n_v, q_v, s_v, u_v, w_v,
     ld, lds, lt, s1, pfr, pgr, rs_, rr, bs, br, zxs, zxr, cs, cr,
@@ -165,35 +167,33 @@
 
     to_smem.wait()
     take(pf, pfr)
-    take(pg, pgr)
-
-    def pack(b, carry):
-        def send(fg, cw):
+
+    def pack(fg):
+        def unit(b, carry):
+            u = n1 * fg + b
+
             def one(c2, carry2):
                 j = tab[(row1, row2)[fg] + b, c2]
                 v = (pf, pg)[fg][jnp.maximum(j, 0)]
-                st[fg, b, c2] = jnp.where(j >= 0, v, 0.0)
+                st[u, c2] = jnp.where(j >= 0, v, 0.0)
                 return carry2
 
             lax.fori_loop(0, nc, one, 0)
-            pltpu.make_async_copy(st.at[fg, b, c], cw.at[b, e, k, c], br.at[fg, b]).start()
+            pltpu.make_async_copy(st.at[u, c], cw.at[u, e, k, c], br.at[u]).start()
 
             def go(d, carry2):
                 c2 = lax.rem(c + d, nc)
-                remote(st.at[fg, b, c2], cw.at[b, e, k, c], bs.at[fg], br.at[fg, b], r, c2).start()
+                remote(st.at[u, c2], cw.at[u, e, k, c], bs, br.at[u], r, c2).start()
                 return carry2
 
             lax.fori_loop(1, nc, go, 0)
-
-        send(0, cw1)
-
-        @pl.when(b < n2)
-        def _():
-            send(1, cw2)
-
-        return carry
-
-    lax.fori_loop(0, n1, pack, 0)
+            return carry
+
+        lax.fori_loop(0, (n1, n2)[fg], unit, 0)
+
+    pack(0)
+    take(pg, pgr)
+    pack(1)
 
     other = z + 1 - 2 * e
     for t in range(4):
@@ -236,114 +236,97 @@
                 part(a, h, down, 0, half), fb.at[h, 1, a, pl.ds(0, half)], r1s, fbr.at[h, 1, a], r, left
             ).start()
 
-    def whole(cw, b):
-        return jnp.concatenate([cw[b, 0].reshape(256, 128), cw[b, 1].reshape(256, 128)], axis=1)
-
-    def weights(b):
-        ff = whole(cw1, b)
+    def weights(u):
+        ff = jnp.concatenate([cw[u, 0].reshape(256, 128), cw[u, 1].reshape(256, 128)], axis=1)
         fh, fl = split(ff)
-        w3[b, 0:256, 0:256] = fh
-        w3[b, 256:512, 0:256] = fl
-        w3[b, 512:768, 0:256] = fh
-        fll = dot3(ff, l_v[...])
-
-        def put(hh):
-            hhi, hlo = split(hh)
-            w3[b, 0:256, 256:512] = hhi
-            w3[b, 256:512, 256:512] = hlo
-            w3[b, 512:768, 256:512] = hhi
-
-        @pl.when(b < n2)
-        def _():
-            put(whole(cw2, jnp.minimum(b, n2 - 1)) - fll)
-
-        @pl.when(b >= n2)
-        def _():
-            put(-fll)
-
-    def term(a, b, lo, cols):
+        w3[u, 0:256] = fh
+        w3[u, 256:512] = fl
+        w3[u, 512:768] = fh
+
+    def term(fg, a, b):
         v = lhs[b, a]
-        return mm(jnp.concatenate([v[:, 0:256], v[:, 0:256], v[:, 256:512]], axis=1), w3[b, :, lo:lo + cols])
-
-    early = n1 - 2
-
-    def part_sums(b):
-        def rowstep(a, cols):
-            got = term(a, b, 0, cols)
-            for fg in range(cols // 256):
-                u = n1 * fg + a
-                g = got[:, fg * 256:fg * 256 + 256].reshape(2, SIDE, SIDE, 8, 256)
+        return mm(jnp.concatenate([v[:, 0:256], v[:, 0:256], v[:, 256:512]], axis=1), w3[n1 * fg + b])
+
+    def shaped(v):
+        return v.reshape(2, SIDE, SIDE, 8, 256)
+
+    def part_sums(fg, b):
+        def one(a, carry):
+            u = n1 * fg + a
+            got = shaped(term(fg, a, b))
+            if fg == 1:
+                acc[u] += got
+            else:
 
                 @pl.when(b == 0)
                 def _():
-                    acc[u] = g
+                    acc[u] = got
 
                 @pl.when(b > 0)
                 def _():
-                    acc[u] += g
-
-        def both(a, carry):
-            rowstep(a, 512)
+                    acc[u] += got
+
             return carry
 
-        def first_only(a, carry):
-            rowstep(a, 256)
+        lax.fori_loop(0, (n1, n2)[fg], one, 0)
+
+    def finish(fg):
+        n = (n1, n2)[fg]
+
+        def one(a, carry):
+            u = n1 * fg + a
+            acc[u] += shaped(term(fg, a, n - 2) + term(fg, a, n - 1))
+            step_one(u)
             return carry
 
-        lax.fori_loop(0, n2, both, 0)
-        if n2 < n1:
-            lax.fori_loop(n2, n1, first_only, 0)
-
-    def finish(fg):
-        def one(a, carry):
-            got = term(a, early, 256 * fg, 256) + term(a, early + 1, 256 * fg, 256)
-            acc[n1 * fg + a] += got.reshape(2, SIDE, SIDE, 8, 256)
-            step_one(n1 * fg + a)
-            return carry
-
-        lax.fori_loop(0, (n1, n2)[fg], one, 0)
-
-    def swap(cw, fg, b):
-        mine = cw.at[b, e, k]
-        take(mine, br.at[fg, b])
-        remote(mine, mine, cs.at[fg], cr.at[fg, b], mate, c).start()
-        remote(mine, mine, zxs.at[fg], zxr.at[fg, b], (z_down, z_up)[fg], c).start()
-
-    def hand(cw, fg, b):
-        got = cw.at[b, 1 - e, k]
-        take(got, zxr.at[fg, b])
-        remote(got, got, cs.at[fg], cr.at[fg, b], mate, c).start()
-
-    def slots(b, carry):
-        @pl.when(b < n1)
+        lax.fori_loop(0, n, one, 0)
+
+    def start_second(a, carry):
+        acc[n1 + a] = shaped(-dot3(acc[a].reshape(256, 256), l_v[...]))
+        return carry
+
+    def swap(u):
+        mine = cw.at[u, e, k]
+        take(mine, br.at[u])
+        remote(mine, mine, cs, cr.at[u], mate, c).start()
+        remote(mine, mine, zxs, zxr.at[u], jnp.where(lax.rem(u, 2) == 0, z_down, z_up), c).start()
+
+    def hand(u):
+        got = cw.at[u, 1 - e, k]
+        take(got, zxr.at[u])
+        remote(got, got, cs, cr.at[u], mate, c).start()
+
+    def units(s, carry):
+        @pl.when(s < nu)
         def _():
-            swap(cw1, 0, b)
-
-        @pl.when(b < n2)
+            swap(s)
+
+        @pl.when(jnp.logical_and(s >= HAND_LAG, s < nu + HAND_LAG))
         def _():
-            swap(cw2, 1, b)
-
-        @pl.when(jnp.logical_and(b > 0, b <= n1))
+            hand(s - HAND_LAG)
+
+        @pl.when(s >= USE_LAG)
         def _():
-            hand(cw1, 0, b - 1)
-
-        @pl.when(jnp.logical_and(b > 0, b <= n2))
-        def _():
-            hand(cw2, 1, b - 1)
-
-        @pl.when(b > 1)
-        def _():
-            take(cw1.at[b - 2, :, 1 - k], cr.at[0, b - 2])
-
-            @pl.when(b - 2 < n2)
+            u = s - USE_LAG
+            take(cw.at[u, :, 1 - k], cr.at[u])
+            weights(u)
+
+            @pl.when(u < n1 - 2)
             def _():
-                take(cw2.at[b - 2, :, 1 - k], cr.at[1, b - 2])
-
-            weights(b - 2)
-
-            @pl.when(b - 2 < early)
+                part_sums(0, u)
+
+            @pl.when(u == n1 - 1)
             def _():
-                part_sums(b - 2)
+                finish(0)
+                lax.fori_loop(0, n2, start_second, 0)
+
+            @pl.when(jnp.logical_and(u >= n1, u < nu - 2))
+            def _():
+                part_sums(1, u - n1)
+
+            @pl.when(u == nu - 1)
+            def _():
+                finish(1)
 
         return carry
 
@@ -358,9 +341,7 @@
         return carry
 
     lax.fori_loop(0, n1 * n1, cast, 0)
-    lax.fori_loop(0, n1 + 2, slots, 0)
-    finish(0)
-    finish(1)
+    lax.fori_loop(0, nu + USE_LAG, units, 0)
 
     def step_two(a, carry):
         for h in range(2):
@@ -523,10 +504,9 @@
 
     take(pf.at[pl.ds(0, (nr - 1) * f1)], s1)
     take(pg.at[pl.ds(0, (nr - 1) * f2)], s1)
-    for fg, cw, n in ((0, cw1, n1), (1, cw2, n2)):
-        take(st.at[fg, pl.ds(0, n), pl.ds(0, nc - 1)], bs.at[fg])
-        take(cw.at[:, :, 0], cs.at[fg])
-        take(cw.at[:, 0, 0], zxs.at[fg])
+    take(st.at[:, pl.ds(0, nc - 1)], bs)
+    take(cw.at[:, :, 0], cs)
+    take(cw.at[:, 0, 0], zxs)
     take(rp.at[pl.ds(0, 3)], rs_)
     take(fb, r1s)
     take(hop, r2s)
@@ -580,8 +560,8 @@
             pltpu.VMEM((32, 128), jnp.int32), pltpu.SMEM((32, 128), jnp.int32),
             vm(na, ns, 256, 256), vm(256, 256), vm(256, 256), vm(256, 256), vm(256, 256),
             vm(nr * f1, 8, 128), vm(nr * f2, 8, 128), vm(4, nu, 8, 128), vm(4, nu, 8, 128),
-            vm(2, n1, nc, 8, 128), vm(n1, 2, 2, nc, 8, 128), vm(n2, 2, 2, nc, 8, 128),
-            pltpu.VMEM((n1, n1, 256, 512), BF16), pltpu.VMEM((n1, 768, 512), BF16),
+            vm(nu, nc, 8, 128), vm(nu, 2, 2, nc, 8, 128),
+            pltpu.VMEM((n1, n1, 256, 512), BF16), pltpu.VMEM((nu, 768, 256), BF16),
             vm(nu, 2, SIDE, SIDE, 8, 256),
             vm(2, 2, nu, half, 8, 256), vm(2, 2, nu, half, 8, 256),
             vm(2, 2, nu, SIDE, 8, 256), vm(2, nu, SIDE, 8, 256),
@@ -591,7 +571,7 @@
             vm(3, nc, 2, 8, 256), vm(3, nc, 8, 256), vm(3, nc, 8, 256), vm(3, nc, 8, 256),
             vm(3, 8, 256), vm(3, nz, 8, 256), vm(2, 3, 8, 256),
             dma((ns,)), dma((3,)), dma, dma, dma, dma, dma, dma,
-            dma((2,)), dma((2, n1)), dma((2,)), dma((2, n1)), dma((2,)), dma((2, n1)),
+            dma, dma((nu,)), dma, dma((nu,)), dma, dma((nu,)),
             dma, dma((2, 2, nu)), dma, dma((2, 2, nu)), dma, dma((2, nu)),
             dma, dma, dma, dma((3,)), dma, dma((3,)), dma, dma((3,)), dma, dma,
         ],

time: 70.3 us -> 67.9 us (0.966)
  Pallas kernels: 68.9 us -> 66.5 us
    pallas_call x1, Pallas kernels: 66.8 us -> 64.4 us  [fused(): pl.pallas_call(functools.partial(kernel, nr, nc, na, ns, f1, f2, n1, n2,...]
where the time goes in v5:
time: 67.9 us; the launch traced here: 67.8 us
  Pallas kernels  66.5 us (98%)
  between operations  1.3 us (2%)
    pallas_call x1, Pallas kernels, fused(): pl.pallas_call(functools.partial(kernel, nr, nc, na, ns, f1, f2, n1, n2,...  64.4 us
    pallas_call x1, Pallas kernels, body(): pl.pallas_call(functools.partial(spread_fits, lax.axis_size('row')), out_...  1.39 us

profile of v5, /device:TPU:1, one launch (start us, length us, event | category | flops | bytes accessed | tf_op | source)
XLA Modules:
  0.0 67.8 jit_solution(7507068900002018400)
XLA Ops:
  0.6 1.4 %shard_map.119 = s32[1]{0:T(128)} custom-call(s32[32]{0:T(128)} %ids1.1, s32[16]{0:T(128)} %ids2.1), custom_call_target="tpu_custom_call" | custom-call | tf_op jit(solution)/shard_map/pallas_call | solution.py:593
  2.7 64.4 %conditional.1 = (f32[208,256]{1,0:T(8,128)S(1)}) conditional(s32[]{:T(128)} %bitcast, (s32[32]{0:T(128)}, s32[16]{0:T(128)}, f32[5,5,256,256]{3,2,1,0:T(8,128)}, f32[2,256,256]{2,1,0:T(8,128)}, f32[1,256,256]{2,1,0:T(8,128)}, /*index=5*/f32[256,256]{1,0:T(8,128)}, f32[256,256]{1,0:T(8,128)}, f32[256,256]{1,0:T(8,128)}) %tuple.18, (s32[32]{0:T(128)}, ...), branch_computations={%region_0.0_spmd, %region_1.0_spmd} | conditional | bytes 8 | solution.py:599
  2.7 64.4 %branch_1_fun.1 = f32[208,256]{1,0:T(8,128)S(1)} custom-call(s32[32]{0:T(128)} %get-tuple-element.43.ids1, s32[16]{0:T(128)} %get-tuple-element.44.ids2, f32[5,5,256,256]{3,2,1,0:T(8,128)} %get-tuple-element.45.inv, f32[2,256,256]{2,1,0:T(8,128)} %get-tuple-element.46.fac1, f32[1,256,256]{2,1,0:T(8,128)} %get-tuple-element.47.fac2, ...), custom_call_target="tpu_custom_call" | custom-call | tf_op jit(solution)/shard_map/cond/branch_1_fun/pallas_call | solution.py:554
  67.1 0.7 %shard_map.120 = (f32[80,256]{1,0:T(8,128)}, f32[80,256]{1,0:T(8,128)}, f32[16,256]{1,0:T(8,128)}, f32[16,256]{1,0:T(8,128)}, f32[16,256]{1,0:T(8,128)}) custom-call(f32[208,256]{1,0:T(8,128)S(1)} %get-tuple-element.66.o), custom_call_target="tpu_custom_call" | custom-call | tf_op jit(solution)/shard_map/pallas_call | solution.py:602

commit v6 on v5

--- a/solution.py
+++ b/solution.py
@@ -37,10 +37,10 @@
     out,
     tab_v, tab, a_v, l_v, d1_v, d2_v, lt_v,
     pf, pg, rps, rp, st, cw, lhs, w3, acc,
-    hop, hopped, fb, ysum, zin, x1b, x2b, frb, grb,
+    hop, hopped, fb, ysum, zin, x1b, x2b, wq,
     st2, rb, m_v, rx, n_v, q_v, s_v, u_v, w_v,
     ld, lds, lt, s1, pfr, pgr, rs_, rr, bs, br, zxs, zxr, cs, cr,
-    r1s, r1r, r2s, fbr, zs, zr, ts, tr, es, er, qs, qr, us, ur, vs, vr,
+    r1s, r1r, r2s, fbr, zs, zr, ws, wr, ts, tr, es, er, qs, qr, us, ur, vs, vr,
 ):
     r = lax.axis_index("row")
     c = lax.axis_index("col")
@@ -63,6 +63,22 @@
             device_id=(row, col), device_id_type=MESH,
         )
 
+    def row_at(i):
+        step = (i + 1) // 2
+        return lax.rem(r + nr // 2 + jnp.where(lax.rem(i, 2) == 1, step, -step), nr)
+
+    def z_at(i):
+        step = (i + 1) // 2
+        return lax.rem(z + nz // 2 + jnp.where(lax.rem(i, 2) == 1, step, -step), nz)
+
+    plane = sorted(
+        ((dy, dx) for dy in range(SIDE) for dx in range(SIDE) if dy or dx),
+        key=lambda v: -(min(v[0], SIDE - v[0]) + min(v[1], SIDE - v[1])),
+    )
+
+    def plane_cols():
+        return [lax.rem(y + dy, SIDE) * SIDE + lax.rem(x + dx, SIDE) for dy, dx in plane]
+
     def take(ref, sem):
         pltpu.make_async_copy(ref, ref, sem).wait()
 
@@ -97,7 +113,7 @@
 
     def send_pieces(fac, buf, count, rsem):
         def go(d, carry):
-            r2 = lax.rem(r + d, nr)
+            r2 = row_at(d)
             k2 = lax.rem(r2, 2)
             rows = pl.multiple_of(128 * k2 + 8 * c, 8)
             side = pl.multiple_of(128 * lax.rem(r2 // 2, 2), 128)
@@ -106,7 +122,7 @@
             ).start()
             return carry
 
-        lax.fori_loop(1, nr, go, 0)
+        lax.fori_loop(0, nr - 1, go, 0)
 
     send_pieces(fac1, pf, f1, pfr)
     send_pieces(fac2, pg, f2, pgr)
@@ -181,12 +197,8 @@
             lax.fori_loop(0, nc, one, 0)
             pltpu.make_async_copy(st.at[u, c], cw.at[u, e, k, c], br.at[u]).start()
 
-            def go(d, carry2):
-                c2 = lax.rem(c + d, nc)
+            for c2 in plane_cols():
                 remote(st.at[u, c2], cw.at[u, e, k, c], bs, br.at[u], r, c2).start()
-                return carry2
-
-            lax.fori_loop(1, nc, go, 0)
             return carry
 
         lax.fori_loop(0, (n1, n2)[fg], unit, 0)
@@ -285,6 +297,18 @@
         acc[n1 + a] = shaped(-dot3(acc[a].reshape(256, 256), l_v[...]))
         return carry
 
+    def row_pieces():
+        take(rp, rr)
+        for h in range(2):
+            v = y if h == 0 else x
+            for u in range(nu):
+                for g in range(2):
+                    wq[h, u, v, :, g * 128:g * 128 + 128] = rp[g * 2 + h, u]
+            for d in range(1, SIDE):
+                v2 = lax.rem(v + d, SIDE)
+                col = v2 * SIDE + x if h == 0 else y * SIDE + v2
+                remote(wq.at[h, :, v], wq.at[h, :, v], ws, wr, r, col).start()
+
     def swap(u):
         mine = cw.at[u, e, k]
         take(mine, br.at[u])
@@ -304,6 +328,10 @@
         @pl.when(jnp.logical_and(s >= HAND_LAG, s < nu + HAND_LAG))
         def _():
             hand(s - HAND_LAG)
+
+        @pl.when(s == USE_LAG - 1)
+        def _():
+            row_pieces()
 
         @pl.when(s >= USE_LAG)
         def _():
@@ -361,18 +389,6 @@
 
     lax.fori_loop(0, nu, step_two, 0)
 
-    take(rp, rr)
-    frb[...] = jnp.zeros_like(frb)
-    grb[...] = jnp.zeros_like(grb)
-    x1b[...] = jnp.zeros_like(x1b)
-    x2b[...] = jnp.zeros_like(x2b)
-    for h in range(2):
-        for g in range(2):
-            for a in range(n1):
-                frb[a * 16 + h * 8:a * 16 + h * 8 + 8, g * 128:g * 128 + 128] = rp[g * 2 + h, a]
-            for a in range(n2):
-                grb[a * 16 + h * 8:a * 16 + h * 8 + 8, g * 128:g * 128 + 128] = rp[g * 2 + h, n1 + a]
-
     def second(a, carry):
         for h in range(2):
             u = ring(h)[0]
@@ -386,7 +402,6 @@
                 remote(ysum.at[h, a, v2], zin.at[h, a, d - 1], zs, zr.at[h, a], r, col).start()
         return carry
 
-    lax.fori_loop(0, nu, second, 0)
 
     def gather(fg, buf):
         def one(a, carry):
@@ -400,11 +415,20 @@
 
         lax.fori_loop(0, (n1, n2)[fg], one, 0)
 
-    gather(0, x1b)
-    x1 = x1b[...]
-    d1t = dot3(jnp.transpose(x1), frb[...]) + d1_v[...]
+    def terms(fg):
+        lo, n = ((0, n1), (n1, n2))[fg]
+        return ysum[:, lo:lo + n].reshape(2 * n * SIDE * 8, 256)
+
+    def own_rows(fg):
+        lo, n = ((0, n1), (n1, n2))[fg]
+        return wq[:, lo:lo + n].reshape(2 * n * SIDE * 8, 256)
+
+    lax.fori_loop(0, n1, second, 0)
+    take(wq.at[:, :, pl.ds(0, SIDE - 1)], wr)
+    d1t = dot3(jnp.transpose(terms(0)), own_rows(0)) + d1_v[...]
     m_v[0] = d1t.reshape(nc, 2, 8, 256)
-    jt = dot3(lt_v[...], d1t) - dot3(jnp.transpose(grb[...]), x1)
+    common = ysum[:, 0:n2].reshape(2 * n2 * SIDE * 8, 256)
+    jt = dot3(lt_v[...], d1t) - dot3(jnp.transpose(own_rows(1)), common)
     m_v[1] = jt.reshape(nc, 2, 8, 256)
 
     def fold(t):
@@ -413,8 +437,8 @@
     fold(0).start()
     fold(1).start()
     base = dot3(jt, l_v[...]) + d2_v[...]
-    gather(1, x2b)
-    et = dot3(jnp.transpose(x2b[...]), grb[...]) + base
+    lax.fori_loop(n1, nu, second, 0)
+    et = dot3(jnp.transpose(terms(1)), own_rows(1)) + base
     m_v[2] = et.reshape(nc, 2, 8, 256)
     fold(2).start()
 
@@ -423,15 +447,14 @@
         n_v[t] = m_v[t, :, k] + rx[t]
         pltpu.make_async_copy(n_v.at[t, c], q_v.at[t, c], qr.at[t]).start()
 
-        def go(d, carry):
-            c2 = lax.rem(c + d, nc)
+        for c2 in plane_cols():
             remote(n_v.at[t, c2], q_v.at[t, c], qs, qr.at[t], r, c2).start()
-            return carry
-
-        lax.fori_loop(1, nc, go, 0)
 
     for t in range(3):
         send_term(t)
+
+    gather(0, x1b)
+    gather(1, x2b)
 
     lane = lax.broadcasted_iota(jnp.int32, (16, 128), 1) // 16
     for c2 in range(nc):
@@ -466,11 +489,11 @@
         pltpu.make_async_copy(s_v.at[t], u_v.at[t, z], ur.at[t]).start()
 
         def go(d, carry):
-            z2 = lax.rem(z + d, nz)
+            z2 = z_at(d)
             remote(s_v.at[t], u_v.at[t, z], us, ur.at[t], z2 * 2 + k, c).start()
             return carry
 
-        lax.fori_loop(1, nz, go, 0)
+        lax.fori_loop(0, nz - 1, go, 0)
 
     for t in range(3):
         send_sum(t)
@@ -511,6 +534,7 @@
     take(fb, r1s)
     take(hop, r2s)
     take(zin, zs)
+    take(wq.at[:, :, pl.ds(0, SIDE - 1)], ws)
     take(rb.at[:, pl.ds(0, nc - 1)], ts)
     take(rx, es)
     take(q_v.at[:, pl.ds(0, nc - 1)], qs)
@@ -566,14 +590,14 @@
             vm(2, 2, nu, half, 8, 256), vm(2, 2, nu, half, 8, 256),
             vm(2, 2, nu, SIDE, 8, 256), vm(2, nu, SIDE, 8, 256),
             vm(2, nu, SIDE - 1, 8, 256),
-            vm(deep, 256), vm(deep, 256), vm(deep, 256), vm(deep, 256),
+            vm(deep, 256), vm(deep, 256), vm(2, nu, SIDE, 8, 256),
             vm(nc, 2, 8, width), vm(2, nc, 8, width),
             vm(3, nc, 2, 8, 256), vm(3, nc, 8, 256), vm(3, nc, 8, 256), vm(3, nc, 8, 256),
             vm(3, 8, 256), vm(3, nz, 8, 256), vm(2, 3, 8, 256),
             dma((ns,)), dma((3,)), dma, dma, dma, dma, dma, dma,
             dma, dma((nu,)), dma, dma((nu,)), dma, dma((nu,)),
             dma, dma((2, 2, nu)), dma, dma((2, 2, nu)), dma, dma((2, nu)),
-            dma, dma, dma, dma((3,)), dma, dma((3,)), dma, dma((3,)), dma, dma,
+            dma, dma, dma, dma, dma, dma((3,)), dma, dma((3,)), dma, dma((3,)), dma, dma,
         ],
         compiler_params=pltpu.CompilerParams(
             collective_id=ident, has_side_effects=True, vmem_limit_bytes=56 * 1024 * 1024

time: 67.9 us -> 62.7 us (0.923)
  Pallas kernels: 66.5 us -> 61.2 us
    pallas_call x1, Pallas kernels: 64.4 us -> 59.1 us  [fused(): pl.pallas_call(functools.partial(kernel, nr, nc, na, ns, f1, f2, n1, n2,...]
where the time goes in v6:
time: 62.7 us; the launch traced here: 62.5 us
  Pallas kernels  61.2 us (98%)
  between operations  1.3 us (2%)
    pallas_call x1, Pallas kernels, fused(): pl.pallas_call(functools.partial(kernel, nr, nc, na, ns, f1, f2, n1, n2,...  59.1 us
    pallas_call x1, Pallas kernels, body(): pl.pallas_call(functools.partial(spread_fits, lax.axis_size('row')), out_...  1.39 us

profile of v6, /device:TPU:1, one launch (start us, length us, event | category | flops | bytes accessed | tf_op | source)
XLA Modules:
  0.0 62.5 jit_solution(12529905919167038177)
XLA Ops:
  0.6 1.4 %shard_map.119 = s32[1]{0:T(128)} custom-call(s32[32]{0:T(128)} %ids1.1, s32[16]{0:T(128)} %ids2.1), custom_call_target="tpu_custom_call" | custom-call | tf_op jit(solution)/shard_map/pallas_call | solution.py:617
  2.7 59.2 %conditional.1 = (f32[208,256]{1,0:T(8,128)S(1)}) conditional(s32[]{:T(128)} %bitcast, (s32[32]{0:T(128)}, s32[16]{0:T(128)}, f32[5,5,256,256]{3,2,1,0:T(8,128)}, f32[2,256,256]{2,1,0:T(8,128)}, f32[1,256,256]{2,1,0:T(8,128)}, /*index=5*/f32[256,256]{1,0:T(8,128)}, f32[256,256]{1,0:T(8,128)}, f32[256,256]{1,0:T(8,128)}) %tuple.18, (s32[32]{0:T(128)}, ...), branch_computations={%region_0.0_spmd, %region_1.0_spmd} | conditional | bytes 8 | solution.py:623
  2.7 59.1 %branch_1_fun.1 = f32[208,256]{1,0:T(8,128)S(1)} custom-call(s32[32]{0:T(128)} %get-tuple-element.43.ids1, s32[16]{0:T(128)} %get-tuple-element.44.ids2, f32[5,5,256,256]{3,2,1,0:T(8,128)} %get-tuple-element.45.inv, f32[2,256,256]{2,1,0:T(8,128)} %get-tuple-element.46.fac1, f32[1,256,256]{2,1,0:T(8,128)} %get-tuple-element.47.fac2, ...), custom_call_target="tpu_custom_call" | custom-call | tf_op jit(solution)/shard_map/cond/branch_1_fun/pallas_call | solution.py:578
  61.9 0.7 %shard_map.120 = (f32[80,256]{1,0:T(8,128)}, f32[80,256]{1,0:T(8,128)}, f32[16,256]{1,0:T(8,128)}, f32[16,256]{1,0:T(8,128)}, f32[16,256]{1,0:T(8,128)}) custom-call(f32[208,256]{1,0:T(8,128)S(1)} %get-tuple-element.66.o), custom_call_target="tpu_custom_call" | custom-call | tf_op jit(solution)/shard_map/pallas_call | solution.py:626
